TPU v7x, 256 devices: a whole 4x4x8 slice. The times are simulated.
256 devices in a mesh: section: 8 (over y, core), dp: 32 (over z, x).
Axes of the slice: x: 4, y: 4, z: 8, core: 2. Of those that a mesh axis runs over, the one named last changes fastest.
Arguments:
- inputs: bfloat16 [5120, 2560], P('dp'), may hold values from -6 to 6
- cotangent: bfloat16 [5120, 2560], P('dp'), may hold values from -6 to 6
- weights: bfloat16 [8, 2560, 2560], P('section', 'dp'), may hold values from -0.0625 to 0.0625
- lengths: int32 [160], P('dp'), may hold values from 1 to 32, as said below
Outputs:
- pre_inputs: bfloat16 [8, 5120, 2560], P('section', 'dp')
- pre_grads: bfloat16 [8, 5120, 2560], P('section', 'dp')
Inputs may be any that keep to these rules, and one draw needn't show every extreme that they name: `lengths`: each micro-batch has at least one live token; some micro-batch is full and some has exactly one.
All inputs are finite; a program needn't handle non-finite values.
Results may differ from a plain program's by a relative error of at most 0.012.
Values may be sent and summed in bfloat16 or wider, within the bound.
No kernel may reach another device: no remote copies, remote signals or barrier semaphores. Data moves between devices by JAX's collectives and lax.ppermute only.
A program may use at most 64 MiB of HBM per device.

v0:
```python
import jax
import jax.numpy as jnp
from jax import lax
from jax.sharding import PartitionSpec as P

BLOCK = 160


epsilon = 1e-05
damping = 0.1


def from_behind(array, axis, by):
    count = lax.axis_size(axis)
    pairs = [(i, i + by) for i in range(count) if 0 <= i + by < count]
    return lax.ppermute(array, axis, pairs)


def normalize(hidden):
    wide = hidden.astype(jnp.float32)
    factor = lax.rsqrt(jnp.mean(wide * wide, axis=-1, keepdims=True) + epsilon)
    return (wide * factor, factor)


def invert_blocks(blocks, counted):
    order = blocks.shape[-1]
    identity = jnp.eye(order, dtype=jnp.float32)
    damped = blocks / counted + damping * identity
    lower = jnp.linalg.cholesky(damped)
    half_way = lax.linalg.triangular_solve(
        lower, jnp.broadcast_to(identity, damped.shape), left_side=True, lower=True
    )
    inverse = lax.linalg.triangular_solve(
        lower, half_way, left_side=True, lower=True, transpose_a=True
    )
    return inverse.astype(jnp.bfloat16)


def apply_blocks(values, inverse):
    shaped = values.reshape(values.shape[0], inverse.shape[0], inverse.shape[1])
    result = jnp.einsum("tbi,bij->tbj", shaped, inverse, preferred_element_type=jnp.float32)
    return result.reshape(1, values.shape[0], values.shape[1]).astype(jnp.bfloat16)


def on_device(inputs, cotangent, weights, lengths):
    section_index = lax.axis_index("section")
    section_count = lax.axis_size("section")
    token_count, width = inputs.shape
    micro_count = lengths.shape[0]
    batch_rows = token_count // micro_count
    moments = micro_count + section_count - 1
    full_weight = lax.all_gather(weights, "dp", axis=1, tiled=True)[0]
    empty = jnp.zeros((batch_rows, width), jnp.bfloat16)
    stored = jnp.zeros((micro_count, batch_rows, width), jnp.bfloat16)

    def forward_moment(moment, carry):
        outgoing, hidden_store = carry
        arrived = from_behind(outgoing, "section", 1)
        position = moment - section_index
        active = jnp.logical_and(position >= 0, position < micro_count)
        picked = jnp.clip(position, 0, micro_count - 1)
        fresh = lax.dynamic_slice_in_dim(inputs, picked * batch_rows, batch_rows, 0)
        current = jnp.where(section_index == 0, fresh, arrived)

        def advance(operands):
            state, kept = operands
            normed, unused = normalize(state)
            activation = normed.astype(jnp.bfloat16)
            result = (
                state.astype(jnp.float32)
                + jnp.dot(activation, full_weight, preferred_element_type=jnp.float32)
            ).astype(jnp.bfloat16)
            return (result, lax.dynamic_update_index_in_dim(kept, state, picked, 0))

        def forward_resting(operands):
            return (jnp.zeros_like(operands[0]), operands[1])

        return lax.cond(active, advance, forward_resting, (current, hidden_store))

    unused_out, hidden_store = lax.fori_loop(0, moments, forward_moment, (empty, stored))

    def backward_moment(moment, carry):
        outgoing, grad_store = carry
        arrived = from_behind(outgoing, "section", -1)
        position = moment - (section_count - 1 - section_index)
        active = jnp.logical_and(position >= 0, position < micro_count)
        picked = jnp.clip(position, 0, micro_count - 1)
        fresh = lax.dynamic_slice_in_dim(cotangent, picked * batch_rows, batch_rows, 0)
        current = jnp.where(section_index == section_count - 1, fresh, arrived)

        def retreat(operands):
            state, kept = operands
            hidden = lax.dynamic_index_in_dim(hidden_store, picked, 0, keepdims=False)
            normed, factor = normalize(hidden)
            back = lax.dot_general(
                state, full_weight, (((1,), (1,)), ((), ())), preferred_element_type=jnp.float32
            )
            through = factor * (back - normed * jnp.mean(back * normed, axis=-1, keepdims=True))
            result = (state.astype(jnp.float32) + through).astype(jnp.bfloat16)
            return (result, lax.dynamic_update_index_in_dim(kept, state, picked, 0))

        def backward_resting(operands):
            return (jnp.zeros_like(operands[0]), operands[1])

        return lax.cond(active, retreat, backward_resting, (current, grad_store))

    unused_back, grad_store = lax.fori_loop(0, moments, backward_moment, (empty, stored))
    activations = normalize(hidden_store.reshape(token_count, width))[0].astype(jnp.bfloat16)
    gradients = grad_store.reshape(token_count, width)
    live = (jnp.arange(batch_rows)[None, :] < lengths[:, None]).reshape(token_count, 1)
    counted = lax.psum(jnp.sum(live.astype(jnp.float32)), "dp")
    blocks_each = width // BLOCK
    zero_value = jnp.zeros((), jnp.bfloat16)
    masked_act = jnp.where(live, activations, zero_value).reshape(token_count, blocks_each, BLOCK)
    masked_grad = jnp.where(live, gradients, zero_value).reshape(token_count, blocks_each, BLOCK)
    gram_act = jnp.einsum(
        "tbi,tbj->bij", masked_act, masked_act, preferred_element_type=jnp.float32
    )
    gram_grad = jnp.einsum(
        "tbi,tbj->bij", masked_grad, masked_grad, preferred_element_type=jnp.float32
    )
    stacked = jnp.concatenate([gram_act, gram_grad], axis=0)
    owned = lax.psum_scatter(stacked, "dp", scatter_dimension=0, tiled=True)
    inverses = lax.all_gather(invert_blocks(owned, counted), "dp", axis=0, tiled=True)
    pre_inputs = apply_blocks(activations, inverses[:blocks_each])
    pre_grads = apply_blocks(gradients, inverses[blocks_each:])
    return (pre_inputs, pre_grads)


def solution(mesh):
    in_specs = (P("dp", None), P("dp", None), P("section", "dp", None), P("dp"))
    out_specs = (P("section", "dp", None), P("section", "dp", None))
    return jax.shard_map(
        on_device, mesh=mesh, in_specs=in_specs, out_specs=out_specs, check_vma=False
    )
```

profile of v0, /device:TPU:2, one launch (start us, length us, event | category | flops | bytes accessed | tf_op | source)
XLA Modules:
  0.0 886.4 jit_solution(7804057373282704373)
XLA Ops:
  8.8 125.0 %all-gather.3.cloned.1.call-done = bf16[1,2560,2560]{2,1,0:T(8,128)(2,1)} async-done(((bf16[1,80,2560]{2,1,0:T(8,128)(2,1)}), bf16[1,2560,2560]{2,1,0:T(8,128)(2,1)}) %all-gather.3.cloned.1.call-update) | async-done | bytes 13107216 | tf_op jit(solution)/shard_map/all_gather | solution.py:52
  134.6 134.8 %while.41 = (s32[]{:T(128)}, bf16[32,2560]{1,0:T(8,128)(2,1)}, bf16[5,32,2560]{2,1,0:T(8,128)(2,1)S(1)}, s32[]{:T(128)}, pred[]{:T(512)}, /*index=5*/bf16[160,25...) while((s32[]{:T(128)}, bf16[32,2560]{1,0:T(8,128)(2,1)}, ...), condition=%wide.region_4.5_spmd, body=%wide.region_0.4_spmd.sunk | while | flops 420249632 | bytes 14910282 | solution.py:80
  137.1 8.9 %conditional.4 = (bf16[32,2560]{1,0:T(8,128)(2,1)}, bf16[5,32,2560]{2,1,0:T(8,128)(2,1)S(1)}) conditional(s32[]{:T(128)} %convert_element_type.167, bf16[5,32,2560]{2,1,0:T(8,128)(2,1)S(1)} %get-tuple-element.714, (pred[]{:T(512)}, s32[]{:T(128)}, bf16[160,2560]{1,0:T(8,128)(2,1)}, bf16[32,2560]{1,0:T(8,128)(2,1)S(1)}, bf16[2560,2560]{1,0:T(8,128)(2,1)}, ...), branch_computations={%region_1.1_spmd, %region_2.3_spmd} | conditional | flops 420249632 | bytes 14254687 | solution.py:78
  148.5 8.9 %conditional.4 = (bf16[32,2560]{1,0:T(8,128)(2,1)}, bf16[5,32,2560]{2,1,0:T(8,128)(2,1)S(1)}) conditional(s32[]{:T(128)} %convert_element_type.167, bf16[5,32,2560]{2,1,0:T(8,128)(2,1)S(1)} %get-tuple-element.714, (pred[]{:T(512)}, s32[]{:T(128)}, bf16[160,2560]{1,0:T(8,128)(2,1)}, bf16[32,2560]{1,0:T(8,128)(2,1)S(1)}, bf16[2560,2560]{1,0:T(8,128)(2,1)}, ...), branch_computations={%region_1.1_spmd, %region_2.3_spmd} | conditional | flops 420249632 | bytes 14254687 | solution.py:78
  160.9 8.9 %conditional.4 = (bf16[32,2560]{1,0:T(8,128)(2,1)}, bf16[5,32,2560]{2,1,0:T(8,128)(2,1)S(1)}) conditional(s32[]{:T(128)} %convert_element_type.167, bf16[5,32,2560]{2,1,0:T(8,128)(2,1)S(1)} %get-tuple-element.714, (pred[]{:T(512)}, s32[]{:T(128)}, bf16[160,2560]{1,0:T(8,128)(2,1)}, bf16[32,2560]{1,0:T(8,128)(2,1)S(1)}, bf16[2560,2560]{1,0:T(8,128)(2,1)}, ...), branch_computations={%region_1.1_spmd, %region_2.3_spmd} | conditional | flops 420249632 | bytes 14254687 | solution.py:78
  174.3 8.9 %conditional.4 = (bf16[32,2560]{1,0:T(8,128)(2,1)}, bf16[5,32,2560]{2,1,0:T(8,128)(2,1)S(1)}) conditional(s32[]{:T(128)} %convert_element_type.167, bf16[5,32,2560]{2,1,0:T(8,128)(2,1)S(1)} %get-tuple-element.714, (pred[]{:T(512)}, s32[]{:T(128)}, bf16[160,2560]{1,0:T(8,128)(2,1)}, bf16[32,2560]{1,0:T(8,128)(2,1)S(1)}, bf16[2560,2560]{1,0:T(8,128)(2,1)}, ...), branch_computations={%region_1.1_spmd, %region_2.3_spmd} | conditional | flops 420249632 | bytes 14254687 | solution.py:78
  190.1 8.9 %conditional.4 = (bf16[32,2560]{1,0:T(8,128)(2,1)}, bf16[5,32,2560]{2,1,0:T(8,128)(2,1)S(1)}) conditional(s32[]{:T(128)} %convert_element_type.167, bf16[5,32,2560]{2,1,0:T(8,128)(2,1)S(1)} %get-tuple-element.714, (pred[]{:T(512)}, s32[]{:T(128)}, bf16[160,2560]{1,0:T(8,128)(2,1)}, bf16[32,2560]{1,0:T(8,128)(2,1)S(1)}, bf16[2560,2560]{1,0:T(8,128)(2,1)}, ...), branch_computations={%region_1.1_spmd, %region_2.3_spmd} | conditional | flops 420249632 | bytes 14254687 | solution.py:78
  206.6 13.9 %collective-permute-start = (bf16[32,2560]{1,0:T(8,128)(2,1)}, bf16[32,2560]{1,0:T(8,128)(2,1)S(1)}, u32[]{:S(2)}, u32[]{:S(2)}) collective-permute-start(bf16[32,2560]{1,0:T(8,128)(2,1)} %get-tuple-element.713), channel_id=1, source_target_pairs={{0,32},{32,64},{64,96},{96,128},{128,160},{160,192},{192,224},{1,3... | collective-permute-start | bytes 491528 | tf_op jit(solution)/shard_map/while/body/eval_jaxpr/ppermute | solution.py:16
  229.8 13.9 %collective-permute-start = (bf16[32,2560]{1,0:T(8,128)(2,1)}, bf16[32,2560]{1,0:T(8,128)(2,1)S(1)}, u32[]{:S(2)}, u32[]{:S(2)}) collective-permute-start(bf16[32,2560]{1,0:T(8,128)(2,1)} %get-tuple-element.713), channel_id=1, source_target_pairs={{0,32},{32,64},{64,96},{96,128},{128,160},{160,192},{192,224},{1,3... | collective-permute-start | bytes 491528 | tf_op jit(solution)/shard_map/while/body/eval_jaxpr/ppermute | solution.py:16
  272.8 231.2 %while.42 = (s32[]{:T(128)}, bf16[32,2560]{1,0:T(8,128)(2,1)}, bf16[5,32,2560]{2,1,0:T(8,128)(2,1)}, s32[]{:T(128)}, pred[]{:T(512)}, /*index=5*/bf16[160,2560]{...) while((s32[]{:T(128)}, bf16[32,2560]{1,0:T(8,128)(2,1)}, ...), condition=%wide.region_11.12_spmd, body=%wide.region_6.11_spmd.sunk | while | flops 420741152 | bytes 16058341 | solution.py:107
  274.1 11.4 %collective-permute-done.1 = bf16[32,2560]{1,0:T(8,128)(2,1)} collective-permute-done((bf16[32,2560]{1,0:T(8,128)(2,1)}, bf16[32,2560]{1,0:T(8,128)(2,1)}, u32[]{:S(2)}, u32[]{:S(2)}) %collective-permute-start.1) | collective-permute-done | bytes 163872 | tf_op jit(solution)/shard_map/while/body/eval_jaxpr/ppermute | solution.py:16
  312.8 11.4 %collective-permute-done.1 = bf16[32,2560]{1,0:T(8,128)(2,1)} collective-permute-done((bf16[32,2560]{1,0:T(8,128)(2,1)}, bf16[32,2560]{1,0:T(8,128)(2,1)}, u32[]{:S(2)}, u32[]{:S(2)}) %collective-permute-start.1) | collective-permute-done | bytes 163872 | tf_op jit(solution)/shard_map/while/body/eval_jaxpr/ppermute | solution.py:16
  342.6 76.5 %collective-permute-done.1 = bf16[32,2560]{1,0:T(8,128)(2,1)} collective-permute-done((bf16[32,2560]{1,0:T(8,128)(2,1)}, bf16[32,2560]{1,0:T(8,128)(2,1)}, u32[]{:S(2)}, u32[]{:S(2)}) %collective-permute-start.1) | collective-permute-done | bytes 163872 | tf_op jit(solution)/shard_map/while/body/eval_jaxpr/ppermute | solution.py:16
  419.1 11.4 %conditional.5 = (bf16[32,2560]{1,0:T(8,128)(2,1)}, bf16[5,32,2560]{2,1,0:T(8,128)(2,1)}) conditional(s32[]{:T(128)} %convert_element_type.168, bf16[5,32,2560]{2,1,0:T(8,128)(2,1)} %get-tuple-element.745, (pred[]{:T(512)}, s32[]{:T(128)}, bf16[160,2560]{1,0:T(8,128)(2,1)}, bf16[32,2560]{1,0:T(8,128)(2,1)}, bf16[5,32,2560]{2,1,0:T(8,128)(2,1)S(1)}, ...), branch_computations={%region_7.7_spmd, %region_8.10_spmd} | conditional | flops 420741152 | bytes 15402730 | solution.py:105
  437.5 11.4 %conditional.5 = (bf16[32,2560]{1,0:T(8,128)(2,1)}, bf16[5,32,2560]{2,1,0:T(8,128)(2,1)}) conditional(s32[]{:T(128)} %convert_element_type.168, bf16[5,32,2560]{2,1,0:T(8,128)(2,1)} %get-tuple-element.745, (pred[]{:T(512)}, s32[]{:T(128)}, bf16[160,2560]{1,0:T(8,128)(2,1)}, bf16[32,2560]{1,0:T(8,128)(2,1)}, bf16[5,32,2560]{2,1,0:T(8,128)(2,1)S(1)}, ...), branch_computations={%region_7.7_spmd, %region_8.10_spmd} | conditional | flops 420741152 | bytes 15402730 | solution.py:105
  455.8 11.4 %conditional.5 = (bf16[32,2560]{1,0:T(8,128)(2,1)}, bf16[5,32,2560]{2,1,0:T(8,128)(2,1)}) conditional(s32[]{:T(128)} %convert_element_type.168, bf16[5,32,2560]{2,1,0:T(8,128)(2,1)} %get-tuple-element.745, (pred[]{:T(512)}, s32[]{:T(128)}, bf16[160,2560]{1,0:T(8,128)(2,1)}, bf16[32,2560]{1,0:T(8,128)(2,1)}, bf16[5,32,2560]{2,1,0:T(8,128)(2,1)S(1)}, ...), branch_computations={%region_7.7_spmd, %region_8.10_spmd} | conditional | flops 420741152 | bytes 15402730 | solution.py:105
  474.2 11.4 %conditional.5 = (bf16[32,2560]{1,0:T(8,128)(2,1)}, bf16[5,32,2560]{2,1,0:T(8,128)(2,1)}) conditional(s32[]{:T(128)} %convert_element_type.168, bf16[5,32,2560]{2,1,0:T(8,128)(2,1)} %get-tuple-element.745, (pred[]{:T(512)}, s32[]{:T(128)}, bf16[160,2560]{1,0:T(8,128)(2,1)}, bf16[32,2560]{1,0:T(8,128)(2,1)}, bf16[5,32,2560]{2,1,0:T(8,128)(2,1)S(1)}, ...), branch_computations={%region_7.7_spmd, %region_8.10_spmd} | conditional | flops 420741152 | bytes 15402730 | solution.py:105
  492.6 11.4 %conditional.5 = (bf16[32,2560]{1,0:T(8,128)(2,1)}, bf16[5,32,2560]{2,1,0:T(8,128)(2,1)}) conditional(s32[]{:T(128)} %convert_element_type.168, bf16[5,32,2560]{2,1,0:T(8,128)(2,1)} %get-tuple-element.745, (pred[]{:T(512)}, s32[]{:T(128)}, bf16[160,2560]{1,0:T(8,128)(2,1)}, bf16[32,2560]{1,0:T(8,128)(2,1)}, bf16[5,32,2560]{2,1,0:T(8,128)(2,1)S(1)}, ...), branch_computations={%region_7.7_spmd, %region_8.10_spmd} | conditional | flops 420741152 | bytes 15402730 | solution.py:105
  517.4 72.4 %psum.7 = f32[]{:T(128)} all-reduce(f32[]{:T(128)} %convert_reduce_fusion), channel_id=1, replica_groups=mesh['section'=8,'dp'=32] {'dp'}, use_global_device_ids=true, to_apply=%region_14.15 | all-reduce | flops 1 | bytes 8 | tf_op jit(solution)/shard_map/psum | solution.py:111
  589.9 147.9 %reduce-scatter.2.cloned.1.call-done = f32[1,160,160]{2,1,0:T(8,128)} async-done(((f32[32,160,160]{2,1,0:T(8,128)}), f32[1,160,160]{2,1,0:T(8,128)}) %reduce-scatter.2.cloned.1.call-update) | async-done | bytes 102416 | tf_op jit(solution)/shard_map/reduce_scatter | solution.py:123
  741.1 11.7 %custom-call.18 = f32[1,128,128]{2,1,0:T(8,128)S(1)} custom-call(f32[1,128,128]{2,1,0:T(8,128)S(1)} %cholesky.120), custom_call_target="Cholesky" | custom-call | tf_op jit(solution)/shard_map/jit(cholesky)/cholesky | solution.py:29
  753.5 9.8 %custom-call.19 = f32[1,1,128,128]{2,3,1,0:T(8,128)S(1)} custom-call(f32[1,1,128,128]{3,2,1,0:T(8,128)S(1)} %get-tuple-element.587), custom_call_target="InvertDiagBlocksLowerTriangular" | custom-call | tf_op jit(solution)/shard_map/jit(cholesky)/cholesky | solution.py:29
  768.7 19.7 %custom-call.21 = f32[1,2,128,128]{2,3,1,0:T(8,128)S(1)} custom-call(f32[1,2,128,128]{3,2,1,0:T(8,128)S(1)} %pad_maximum_fusion.1), custom_call_target="InvertDiagBlocksLowerTriangular" | custom-call | tf_op jit(solution)/shard_map/triangular_solve | solution.py:33
  790.9 76.6 %all-gather.5.cloned.1.call-done = bf16[32,160,160]{2,1,0:T(8,128)(2,1)} async-done(((bf16[1,160,160]{2,1,0:T(8,128)(2,1)}), bf16[32,160,160]{2,1,0:T(8,128)(2,1)}) %all-gather.5.cloned.1.call-update) | async-done | bytes 1638416 | tf_op jit(solution)/shard_map/all_gather | solution.py:124
  (177 shorter events, 289.7 us)
Async XLA Ops:
  7.2 126.6 %all-gather.3.cloned.1.call-start = ((), (), s32[]{:S(2)}) async-start(), calls=%async_computation.1 | async-start | bytes 13516800 | tf_op jit(solution)/shard_map/all_gather | solution.py:52
  7.9 729.9 %reduce-scatter.2.cloned.1.call-start = ((), (), s32[]{:S(2)}) async-start(), calls=%async_computation.2 | async-start | bytes 5406720 | tf_op jit(solution)/shard_map/reduce_scatter | solution.py:123
  169.9 4.5 collective-permute-start
  183.3 6.8 collective-permute-start
  199.0 6.8 collective-permute-start
  206.6 15.1 %collective-permute-start = (bf16[32,2560]{1,0:T(8,128)(2,1)}, bf16[32,2560]{1,0:T(8,128)(2,1)S(1)}, u32[]{:S(2)}, u32[]{:S(2)}) collective-permute-start(bf16[32,2560]{1,0:T(8,128)(2,1)} %get-tuple-element.713), channel_id=1, source_target_pairs={{0,32},{32,64},{64,96},{96,128},{128,160},{160,192},{192,224},{1,3... | collective-permute-start | bytes 491528 | tf_op jit(solution)/shard_map/while/body/eval_jaxpr/ppermute | solution.py:16
  222.3 6.8 collective-permute-start
  229.8 15.1 %collective-permute-start = (bf16[32,2560]{1,0:T(8,128)(2,1)}, bf16[32,2560]{1,0:T(8,128)(2,1)S(1)}, u32[]{:S(2)}, u32[]{:S(2)}) collective-permute-start(bf16[32,2560]{1,0:T(8,128)(2,1)} %get-tuple-element.713), channel_id=1, source_target_pairs={{0,32},{32,64},{64,96},{96,128},{128,160},{160,192},{192,224},{1,3... | collective-permute-start | bytes 491528 | tf_op jit(solution)/shard_map/while/body/eval_jaxpr/ppermute | solution.py:16
  245.6 6.8 collective-permute-start
  253.1 8.0 collective-permute-start
  261.8 6.8 collective-permute-start
  272.8 12.7 %collective-permute-start.1 = (bf16[32,2560]{1,0:T(8,128)(2,1)}, bf16[32,2560]{1,0:T(8,128)(2,1)}, u32[]{:S(2)}, u32[]{:S(2)}) collective-permute-start(bf16[32,2560]{1,0:T(8,128)(2,1)} %get-tuple-element.744), channel_id=1, source_target_pairs={{32,0},{64,32},{96,64},{128,96},{160,128},{192,160},{224,192},{33,... | collective-permute-start | bytes 491528 | tf_op jit(solution)/shard_map/while/body/eval_jaxpr/ppermute | solution.py:16
  286.2 7.6 collective-permute-start.1
  294.5 8.0 collective-permute-start.1
  303.2 7.6 collective-permute-start.1
  311.5 12.7 %collective-permute-start.1 = (bf16[32,2560]{1,0:T(8,128)(2,1)}, bf16[32,2560]{1,0:T(8,128)(2,1)}, u32[]{:S(2)}, u32[]{:S(2)}) collective-permute-start(bf16[32,2560]{1,0:T(8,128)(2,1)} %get-tuple-element.744), channel_id=1, source_target_pairs={{32,0},{64,32},{96,64},{128,96},{160,128},{192,160},{224,192},{33,... | collective-permute-start | bytes 491528 | tf_op jit(solution)/shard_map/while/body/eval_jaxpr/ppermute | solution.py:16
  324.9 7.6 collective-permute-start.1
  333.2 7.4 collective-permute-start.1
  341.3 77.8 %collective-permute-start.1 = (bf16[32,2560]{1,0:T(8,128)(2,1)}, bf16[32,2560]{1,0:T(8,128)(2,1)}, u32[]{:S(2)}, u32[]{:S(2)}) collective-permute-start(bf16[32,2560]{1,0:T(8,128)(2,1)} %get-tuple-element.744), channel_id=1, source_target_pairs={{32,0},{64,32},{96,64},{128,96},{160,128},{192,160},{224,192},{33,... | collective-permute-start | bytes 491528 | tf_op jit(solution)/shard_map/while/body/eval_jaxpr/ppermute | solution.py:16
  430.5 6.9 collective-permute-start.1
  448.9 6.9 collective-permute-start.1
  467.3 6.9 collective-permute-start.1
  485.7 6.9 collective-permute-start.1
  516.1 351.4 %all-gather.5.cloned.1.call-start = ((), (), s32[]{:S(2)}) async-start(), calls=%async_computation.3 | async-start | bytes 2703360 | tf_op jit(solution)/shard_map/all_gather | solution.py:124
  (4 other events, 9.2 us)
Sparse Core Ops, SparseCore 0:
  10.6 123.2 all-gather.2
  516.3 221.5 reduce-scatter.1
  791.0 76.4 all-gather.4
where the time goes:
time: 889 us; the launch traced here: 886 us
  waiting for transfers between devices  518 us (58%)
  matrix products  98.3 us (11%)
  starting transfers between devices  86.2 us (10%)
  blocking collectives  72.4 us (8%)
  other arithmetic  72.1 us (8%)
  local copies, waits for them, and re-layouts  23.1 us (3%)
  between operations  15.3 us (2%)
    ppermute x24, waiting for transfers between devices, from_behind(): return lax.ppermute(array, axis, pairs)  168 us
    reduce_scatter x1, waiting for transfers between devices, on_device(): owned = lax.psum_scatter(stacked, 'dp', scatter_dimension=0, tiled=True)  148 us
    all_gather x1, waiting for transfers between devices, on_device(): full_weight = lax.all_gather(weights, 'dp', axis=1, tiled=True)[0]  125 us
    ppermute x24, starting transfers between devices, from_behind(): return lax.ppermute(array, axis, pairs)  86.1 us
    all_gather x1, waiting for transfers between devices, on_device(): lax.all_gather(invert_blocks(owned, counted), 'dp', axis=0, tiled=True)  76.6 us
    psum x1, blocking collectives, on_device(): counted = lax.psum(jnp.sum(live.astype(jnp.float32)), 'dp')  72.4 us
    dot_general x5, matrix products, retreat(): lax.dot_general(state, full_weight, (((1,), (1,)), ((), ())), preferred_e...  43.6 us
    dot_general x5, matrix products, advance(): jnp.dot(activation, full_weight, preferred_element_type=jnp.float32)  39.1 us
  transfers between devices with their start and end apart: 27, of which 27 were waited for; matrix products, arithmetic and copies ran while one was open for 0% of the time, Pallas kernels for 0%

commit v1 on v0

v1 whole, which is shorter than its diff:
```python
import jax
import jax.numpy as jnp
from jax import lax
from jax.experimental import pallas as pl
from jax.experimental.pallas import tpu as pltpu
from jax.sharding import PartitionSpec as P

BLOCK = 160
EPSILON = 1e-05
DAMPING = 0.1
LANES = 128
TILE = 256

f32 = jnp.float32
bf16 = jnp.bfloat16


def row_factor(own, other, width):
    total = jnp.sum(own * own, axis=-1, keepdims=True)
    total = total + jnp.sum(other * other, axis=-1, keepdims=True)
    return lax.rsqrt(total / width + EPSILON)


def forward_kernel(core_ref, own_ref, other_ref, wown_ref, wother_ref, out_ref, aown, aother):
    step = pl.program_id(0)
    half = own_ref.shape[1]

    @pl.when(step == 0)
    def _():
        own = own_ref[...].astype(f32)
        other = other_ref[...].astype(f32)
        factor = row_factor(own, other, 2 * half)
        aown[...] = (own * factor).astype(bf16)
        aother[...] = (other * factor).astype(bf16)

    result = jnp.dot(aown[...], wown_ref[...], preferred_element_type=f32)
    result = result + jnp.dot(aother[...], wother_ref[...], preferred_element_type=f32)
    columns = pl.ds(pl.multiple_of(step * TILE, TILE), TILE)
    out_ref[...] = (own_ref[:, columns].astype(f32) + result).astype(bf16)


def forward_layer(core, own, other, weight, which):
    rows, half = own.shape
    steps = half // TILE
    whole = pl.BlockSpec((rows, half), lambda i, c: (0, 0))
    return pl.pallas_call(
        forward_kernel,
        out_shape=jax.ShapeDtypeStruct((rows, half), bf16),
        grid_spec=pltpu.PrefetchScalarGridSpec(
            num_scalar_prefetch=1,
            grid=(steps,),
            in_specs=[
                whole,
                whole,
                pl.BlockSpec((half, TILE), lambda i, c: (c[0], which * steps + i)),
                pl.BlockSpec((half, TILE), lambda i, c: (1 - c[0], which * steps + i)),
            ],
            out_specs=pl.BlockSpec((rows, TILE), lambda i, c: (0, i)),
            scratch_shapes=[pltpu.VMEM((rows, half), bf16), pltpu.VMEM((rows, half), bf16)],
        ),
        cost_estimate=pl.CostEstimate(
            flops=4 * rows * half * half, bytes_accessed=4 * half * half, transcendentals=0
        ),
    )(core, own, other, weight, weight)


def backward_kernel(core_ref, grad_ref, own_ref, other_ref, weight_ref, send_ref, keep_ref, factor):
    step = pl.program_id(0)
    half = own_ref.shape[1]
    steps = half // TILE

    @pl.when(step == 0)
    def _():
        own = own_ref[...].astype(f32)
        other = other_ref[...].astype(f32)
        factor[...] = jnp.broadcast_to(row_factor(own, other, 2 * half), factor.shape)
        send_ref[:, half:] = jnp.zeros((own.shape[0], LANES), f32)

    part = lax.dot_general(
        grad_ref[...], weight_ref[...], (((1,), (1,)), ((), ())), preferred_element_type=f32
    )

    def along(hidden_ref, columns):
        product = part * hidden_ref[:, columns].astype(f32)
        send_ref[:, half:] += (product[:, :LANES] + product[:, LANES:]) * factor[...]

    @pl.when(step < steps)
    def _():
        columns = pl.ds(pl.multiple_of(step * TILE, TILE), TILE)
        along(other_ref, columns)
        send_ref[:, columns] = part

    @pl.when(step >= steps)
    def _():
        columns = pl.ds(pl.multiple_of((step - steps) * TILE, TILE), TILE)
        along(own_ref, columns)
        keep_ref[:, columns] = part


def backward_layer(core, grad, own, other, weight, which):
    rows, half = own.shape
    steps = half // TILE
    whole = pl.BlockSpec((rows, half), lambda i, c: (0, 0))

    def place(i, c):
        return (jnp.where(i < steps, (1 - c[0]) * steps + i, c[0] * steps + i - steps), which)

    send, keep = pl.pallas_call(
        backward_kernel,
        out_shape=[
            jax.ShapeDtypeStruct((rows, half + LANES), f32),
            jax.ShapeDtypeStruct((rows, half), f32),
        ],
        grid_spec=pltpu.PrefetchScalarGridSpec(
            num_scalar_prefetch=1,
            grid=(2 * steps,),
            in_specs=[whole, whole, whole, pl.BlockSpec((TILE, half), place)],
            out_specs=[pl.BlockSpec((rows, half + LANES), lambda i, c: (0, 0)), whole],
            scratch_shapes=[pltpu.VMEM((rows, LANES), f32)],
        ),
        cost_estimate=pl.CostEstimate(
            flops=4 * rows * half * half, bytes_accessed=4 * half * half, transcendentals=0
        ),
    )(core, grad, own, other, weight)
    arrived = swap_cores(send)
    width = 2 * half
    wide_own, wide_other = own.astype(f32), other.astype(f32)
    factor = row_factor(wide_own, wide_other, width)
    mean = jnp.sum(send[:, half:] + arrived[:, half:], axis=-1, keepdims=True) / width
    back = keep + arrived[:, :half]
    through = factor * (back - wide_own * factor * mean)
    return (grad.astype(f32) + through).astype(bf16)


PANEL = 32


def inverse_kernel(gram_ref, count_ref, out_ref, work):
    many, order = work.shape[0], work.shape[1]
    counted = count_ref[0]
    rows = lax.broadcasted_iota(jnp.int32, (order, order), 0)
    columns = lax.broadcasted_iota(jnp.int32, (order, order), 1)
    small_rows = lax.broadcasted_iota(jnp.int32, (PANEL, PANEL), 0)
    small_columns = lax.broadcasted_iota(jnp.int32, (PANEL, PANEL), 1)
    for m in range(many):
        total = gram_ref[0, m]
        for part in range(1, gram_ref.shape[0]):
            total = total + gram_ref[part, m]
        work[m] = total / counted + jnp.where(rows == columns, DAMPING, 0.0)
    for start in range(0, order, PANEL):
        stop = start + PANEL
        strips = [work[m, start:stop, :] for m in range(many)]
        pivots = [strip[:, start:stop] for strip in strips]
        for k in range(PANEL):
            keep = (small_rows != k) & (small_columns != k)
            for m in range(many):
                block = pivots[m]
                pivot = block[k : k + 1, k : k + 1]
                row = jnp.where(small_columns[:1] == k, -1.0, block[k : k + 1, :])
                column = jnp.where(small_rows[:, :1] == k, -1.0, block[:, k : k + 1])
                pivots[m] = jnp.where(keep, block, 0.0) - column * (row / pivot)
        inside_row = (rows >= start) & (rows < stop)
        inside_column = (columns >= start) & (columns < stop)
        strip_column = inside_column[:PANEL]
        unit = small_rows_eye(small_rows, columns[:PANEL], start)
        for m in range(many):
            strip = jnp.where(strip_column, unit, strips[m])
            solved = jnp.dot(
                -pivots[m], strip, precision=lax.Precision.HIGHEST, preferred_element_type=f32
            )
            change = lax.dot_general(
                strip,
                solved,
                (((0,), (0,)), ((), ())),
                precision=lax.Precision.HIGHEST,
                preferred_element_type=f32,
            )
            work[m] = jnp.where(inside_row | inside_column, 0.0, work[m]) - change
    for m in range(many):
        out_ref[m] = (-work[m]).astype(bf16)


def small_rows_eye(small_rows, wide_columns, start):
    rows = lax.broadcasted_iota(jnp.int32, wide_columns.shape, 0)
    return jnp.where(wide_columns == rows + start, -1.0, 0.0)


def invert_blocks(parts, counted):
    many, order = parts.shape[1], parts.shape[2]
    return pl.pallas_call(
        inverse_kernel,
        out_shape=jax.ShapeDtypeStruct((many, order, order), bf16),
        in_specs=[
            pl.BlockSpec(memory_space=pltpu.VMEM),
            pl.BlockSpec(memory_space=pltpu.SMEM),
        ],
        out_specs=pl.BlockSpec(memory_space=pltpu.VMEM),
        scratch_shapes=[pltpu.VMEM((many, order, order), f32)],
    )(parts, counted)


def swap_cores(array):
    count = lax.axis_size("section")
    return lax.ppermute(array, "section", [(i, i ^ 1) for i in range(count)])


def hop(array, source, by):
    pairs = [(2 * source + core, 2 * (source + by) + core) for core in range(2)]
    return lax.ppermute(array, "section", pairs)


def groups_along(count, stride, length):
    return [
        [base + stride * k for k in range(length)]
        for base in range(count)
        if (base // stride) % length == 0
    ]


def halves(core, own, other):
    first = jnp.where(core == 0, own, other)
    second = jnp.where(core == 0, other, own)
    return jnp.concatenate([first, second], axis=1)


def spread(values):
    lines = groups_along(lax.axis_size("dp"), 4, 8)
    return lax.all_to_all(
        values, "dp", split_axis=1, concat_axis=0, axis_index_groups=lines, tiled=True
    )


def gather_back(values):
    lines = groups_along(lax.axis_size("dp"), 4, 8)
    return lax.all_to_all(
        values, "dp", split_axis=0, concat_axis=1, axis_index_groups=lines, tiled=True
    )


def gram_parts(taken, live):
    blocks = taken.shape[1] // BLOCK
    masked = jnp.where(live, taken, jnp.zeros((), bf16))
    grams = []
    for b in range(blocks):
        part = masked[:, b * BLOCK : (b + 1) * BLOCK]
        grams.append(
            lax.dot_general(part, part, (((0,), (0,)), ((), ())), preferred_element_type=f32)
        )
    mates = groups_along(lax.axis_size("dp"), 1, 4)
    return lax.all_gather(jnp.stack(grams), "dp", axis=0, axis_index_groups=mates)


def apply_blocks(taken, inverse):
    blocks = inverse.shape[0]
    results = [
        jnp.dot(
            taken[:, b * BLOCK : (b + 1) * BLOCK], inverse[b], preferred_element_type=f32
        ).astype(bf16)
        for b in range(blocks)
    ]
    return jnp.concatenate(results, axis=1)


def on_device(inputs, cotangent, weights, lengths):
    section = lax.axis_index("section")
    chip, core = section // 2, section % 2
    chips = lax.axis_size("section") // 2
    tokens, width = inputs.shape
    half = width // 2
    batch_rows = tokens // lengths.shape[0]
    scalar_core = core.reshape(1).astype(jnp.int32)

    local = weights[0]
    mine = jnp.where(core == 0, local[:, :half], local[:, half:])
    theirs = jnp.where(core == 0, local[:, half:], local[:, :half])
    swapped = swap_cores(theirs)
    paired = halves(core, mine, swapped)
    weight = lax.all_gather(paired, "dp", axis=0, tiled=True)

    all_lengths = lax.all_gather(lengths, "dp", axis=0)
    alive = jnp.clip(all_lengths, 0, batch_rows)
    counted = jnp.sum(alive).astype(f32).reshape(1)
    across = lax.axis_index("dp") % 4
    line = lax.dynamic_index_in_dim(all_lengths.reshape(8, 4, -1), across, 1, keepdims=False)
    live = (jnp.arange(batch_rows)[None, :] < line.reshape(-1, 1)).reshape(-1, 1)

    def own_half(array):
        return jnp.where(core == 0, array[:, :half], array[:, half:])

    def other_half(array):
        return jnp.where(core == 0, array[:, half:], array[:, :half])

    first_own = own_half(inputs)
    empty = jnp.zeros((tokens, half), bf16)
    kept = (empty, empty, empty, empty)
    arriving = first_own
    for stage in range(chips):
        last = stage == chips - 1

        def turn(operands, stage=stage, last=last):
            own, weight = operands
            other = other_half(inputs) if stage == 0 else swap_cores(own)
            second = forward_layer(scalar_core, own, other, weight, 0)
            second_other = swap_cores(second)
            if last:
                leaving = empty
            else:
                leaving = forward_layer(scalar_core, second, second_other, weight, 1)
            return (own, other, second, second_other), leaving

        def rest(operands, kept=kept):
            return kept, empty

        kept, leaving = lax.cond(chip == stage, turn, rest, (arriving, weight))
        if not last:
            arriving = hop(leaving, stage, 1)

    own_a, other_a, own_b, other_b = kept
    grads = (empty, empty)
    arriving = own_half(cotangent)
    pre_inputs = None
    taken = None
    for stage in range(chips - 1, -1, -1):

        def turn(operands, stage=stage):
            grad, own_a, other_a, own_b, other_b, weight = operands
            grad_a = backward_layer(scalar_core, grad, own_b, other_b, weight, 1)
            if stage == 0:
                leaving = empty
            else:
                leaving = backward_layer(scalar_core, grad_a, own_a, other_a, weight, 0)
            return (grad_a, grad), leaving

        def rest(operands, grads=grads):
            return grads, empty

        grads, leaving = lax.cond(
            chip == stage, turn, rest, (arriving, own_a, other_a, own_b, other_b, weight)
        )
        if stage > 0:
            arriving = hop(leaving, stage, -1)
        if stage == chips - 1:
            own = jnp.where(core == 0, own_a, own_b)
            other = jnp.where(core == 0, other_a, other_b)
            own, other, leaving = lax.optimization_barrier((own, other, leaving))
            full = halves(core, own, other).astype(f32)
            mean = jnp.mean(full * full, axis=-1, keepdims=True)
            taken = spread((full * lax.rsqrt(mean + EPSILON)).astype(bf16))
            parts = gram_parts(taken, live)
            arriving, parts = lax.optimization_barrier((arriving, parts))
        elif stage == chips - 2:
            grads, parts = lax.optimization_barrier((grads, parts))
            inverse = invert_blocks(parts, counted)
            pre_inputs = gather_back(apply_blocks(taken, inverse))
            arriving, pre_inputs = lax.optimization_barrier((arriving, pre_inputs))

    grad_a, grad_b = grads
    own = jnp.where(core == 0, grad_a, grad_b)
    other = swap_cores(jnp.where(core == 0, grad_b, grad_a))
    taken = spread(halves(core, own, other))
    inverse = invert_blocks(gram_parts(taken, live), counted)
    pre_grads = gather_back(apply_blocks(taken, inverse))
    return (pre_inputs[None], pre_grads[None])


def solution(mesh):
    in_specs = (P("dp", None), P("dp", None), P("section", "dp", None), P("dp"))
    out_specs = (P("section", "dp", None), P("section", "dp", None))
    return jax.shard_map(
        on_device, mesh=mesh, in_specs=in_specs, out_specs=out_specs, check_vma=False
    )
```

time: 889 us -> 566 us (0.64)
  waiting for transfers between devices: 518 us -> 309 us
  matrix products: 98.3 us -> 7.58 us
  starting transfers between devices: 86.2 us -> 14.6 us
  Pallas kernels: 0 us -> 58.3 us
  other arithmetic: 72.1 us -> 14.7 us
  blocking collectives: 72.4 us -> 123 us
  local copies, waits for them, and re-layouts: 23.1 us -> 11.5 us
    reduce_scatter x1 -> x0, waiting for transfers between devices: 148 us -> none  [on_device(): owned = lax.psum_scatter(stacked, 'dp', scatter_dimension=0, tiled=True)]
    dot_general x14 -> x8, matrix products: 96.5 us -> 7.58 us  [the longest x4 5.43 us: apply_blocks(): jnp.dot(taken[:, b * BLOCK:(b + 1) * BLOCK], inverse[b], preferred_elemen...]
    ppermute x24 -> x10, starting transfers between devices: 86.1 us -> 5.67 us  [the longest x6 5.34 us: hop(): return lax.ppermute(array, 'section', pairs)]
    all_gather x2 -> x1, waiting for transfers between devices: 202 us -> 123 us  [on_device(): weight = lax.all_gather(paired, 'dp', axis=0, tiled=True)]
    psum x1 -> x0, blocking collectives: 72.4 us -> none  [on_device(): counted = lax.psum(jnp.sum(live.astype(jnp.float32)), 'dp')]
    all_to_all x0 -> x2, blocking collectives: none -> 61.2 us  [the longest x1 34.4 us: spread(): lax.all_to_all(values, 'dp', split_axis=1, concat_axis=0, axis_index_grou...]
    pallas_call x0 -> x5, Pallas kernels: none -> 58.3 us  [the longest x2 36.4 us: invert_blocks(): pl.pallas_call(inverse_kernel, out_shape=jax.ShapeDtypeStruct((many, orde...]
    another operation x15 -> x2, other arithmetic: 45.6 us -> 0.05 us  [gram_parts(): jnp.stack(grams)]
  transfers between devices with their start and end apart: 27 -> 13, of which waited for: 27 -> 8; matrix products, arithmetic and copies ran while one was open for 0% -> 1% of each run, Pallas kernels for 0% -> 0%
where the time goes in v1:
time: 566 us; the launch traced here: 556 us
  waiting for transfers between devices  309 us (55%)
  blocking collectives  123 us (22%)
  Pallas kernels  58.3 us (10%)
  between operations  16 us (3%)
  other arithmetic  14.7 us (3%)
  starting transfers between devices  14.6 us (3%)
  local copies, waits for them, and re-layouts  11.5 us (2%)
  matrix products  7.58 us (1%)
    ppermute x6, waiting for transfers between devices, hop(): return lax.ppermute(array, 'section', pairs)  156 us
    all_gather x1, waiting for transfers between devices, on_device(): weight = lax.all_gather(paired, 'dp', axis=0, tiled=True)  123 us
    pallas_call x2, Pallas kernels, invert_blocks(): pl.pallas_call(inverse_kernel, out_shape=jax.ShapeDtypeStruct((many, orde...  36.4 us
    all_to_all x1, blocking collectives, spread(): lax.all_to_all(values, 'dp', split_axis=1, concat_axis=0, axis_index_grou...  34.4 us
    all_gather x2, blocking collectives, gram_parts(): lax.all_gather(jnp.stack(grams), 'dp', axis=0, axis_index_groups=mates)  32.4 us
    unnamed x1, blocking collectives  29.3 us
    all_to_all x1, blocking collectives, gather_back(): lax.all_to_all(values, 'dp', split_axis=0, concat_axis=1, axis_index_grou...  26.8 us
    all_to_all x1, waiting for transfers between devices, gather_back(): lax.all_to_all(values, 'dp', split_axis=0, concat_axis=1, axis_index_grou...  24 us
  transfers between devices with their start and end apart: 13, of which 8 were waited for; matrix products, arithmetic and copies ran while one was open for 1% of the time, Pallas kernels for 0%

profile of v1, /device:TPU:2, one launch (start us, length us, event | category | flops | bytes accessed | tf_op | source)
XLA Modules:
  0.0 555.7 jit_solution(4983275177104101491)
XLA Ops:
  11.8 123.4 %all-gather.5.cloned.1.call-done = bf16[2560,2560]{1,0:T(8,128)(2,1)} async-done(((bf16[80,2560]{1,0:T(8,128)(2,1)}), bf16[2560,2560]{1,0:T(8,128)(2,1)}) %all-gather.5.cloned.1.call-update) | async-done | bytes 13107216 | tf_op jit(solution)/shard_map/all_gather | solution.py:278
  135.2 15.1 %conditional.8 = (bf16[160,1280]{1,0:T(8,128)(2,1)S(1)}, bf16[160,1280]{1,0:T(8,128)(2,1)}, bf16[160,1280]{1,0:T(8,128)(2,1)}, bf16[160,1280]{1,0:T(8,128)(2,1)}, bf16[160,1280]{1,0:T(8,128)(2,1)S(1)}) conditional(s32[]{:T(128)} %convert_element_type.128, () %tuple.75, (pred[]{:T(512)}, bf16[160,2560]{1,0:T(8,128)(2,1)S(1)}, s32[]{:T(128)}, ...), branch_computations={%region_0.1_spmd, %region_1.2_spmd} | conditional | flops 2097561600 | bytes 19660948 | solution.py:314
  136.0 6.4 %branch_1_fun.14.own_ref = bf16[160,1280]{1,0:T(8,128)(2,1)} custom-call(s32[1]{0:T(128)} %get-tuple-element.132.core_ref, bf16[160,1280]{1,0:T(8,128)(2,1)S(1)} %get-tuple-element.309.own_ref, bf16[160,1280]{1,0:T(8,128)(2,1)} %get-tuple-element.310.other_ref, bf16[2560,2560]{1,0:T(8,128)(2,1)} %get-tuple-element.133.wown_ref.wother_ref, ...), custom_call_target="tpu_custom_call" | custom-call | flops 1048576000 | bytes 6553600 | tf_op jit(solution)/shard_map/cond/branch_1_fun/pallas_call | solution.py:46
  142.4 2.1 collective-permute-done.6.other_ref
  144.5 5.7 %branch_1_fun.15 = bf16[160,1280]{1,0:T(8,128)(2,1)S(1)} custom-call(s32[1]{0:T(128)} %get-tuple-element.132.core_ref, bf16[160,1280]{1,0:T(8,128)(2,1)} %branch_1_fun.14.own_ref, bf16[160,1280]{1,0:T(8,128)(2,1)} %collective-permute-done.6.other_ref, bf16[2560,2560]{1,0:T(8,128)(2,1)} %get-tuple-element.133.wown_ref.wother_ref, ...), custom_call_target="tpu_custom_call" | custom-call | flops 1048576000 | bytes 6553600 | tf_op jit(solution)/shard_map/cond/branch_1_fun/pallas_call | solution.py:46
  151.6 9.3 %collective-permute-done.15 = bf16[160,1280]{1,0:T(8,128)(2,1)S(1)} collective-permute-done((bf16[160,1280]{1,0:T(8,128)(2,1)S(1)}, bf16[160,1280]{1,0:T(8,128)(2,1)S(1)}, u32[]{:S(2)}, u32[]{:S(2)}) %collective-permute-start.15) | collective-permute-done | bytes 409632 | tf_op jit(solution)/shard_map/ppermute | solution.py:209
  163.6 1.8 conditional.12
  168.4 4.4 all-to-all-start
  174.2 29.3 %all-reduce = s32[160]{0:T(256)S(1)} all-reduce(s32[160]{0:T(256)S(1)} %dynamic-update-slice), channel_id=2, replica_groups=mesh['section'=8,'dp'=32] {'dp'}, use_global_device_ids=true, to_apply=%add | all-reduce | flops 160 | bytes 1280
  207.3 16.3 %all-gather.1 = f32[8,160,160]{2,1,0:T(8,128)} all-gather(f32[2,160,160]{2,1,0:T(8,128)S(1)} %pad_maximum_fusion.4), channel_id=3, replica_groups={{0,1,2,3},{4,5,6,7},{8,9,10,11},{12,13,14,15},{16,17,18,19},{20,21,22,2..., dimensions={0}, use_global_device_ids=true | all-gather | bytes 1024000 | tf_op jit(solution)/shard_map/all_gather | solution.py:250
  224.0 18.2 %shard_map.61 = bf16[2,160,160]{2,1,0:T(8,128)(2,1)} custom-call(f32[4,2,160,160]{3,2,1,0:T(8,128)} %bitcast.43, f32[1]{0:T(128)} %bitcast.9.count_ref), custom_call_target="tpu_custom_call" | custom-call | tf_op jit(solution)/shard_map/pallas_call | solution.py:190
  246.3 4.5 all-to-all-start.1
  251.5 24.0 %all-to-all-done.1 = bf16[8,160,320]{2,1,0:T(8,128)(2,1)S(1)} async-done(((bf16[8,160,320]{2,1,0:T(8,128)(2,1)}), bf16[8,160,320]{2,1,0:T(8,128)(2,1)S(1)}, u32[]{:S(2)}, u32[]{:S(2)}) %all-to-all-start.1) | async-done | bytes 819232 | tf_op jit(solution)/shard_map/all_to_all | solution.py:235
  275.8 1.5 all_to_all.58
  278.7 147.0 %collective-permute-done.20 = bf16[160,1280]{1,0:T(8,128)(2,1)S(1)} collective-permute-done((bf16[160,1280]{1,0:T(8,128)(2,1)S(1)}, bf16[160,1280]{1,0:T(8,128)(2,1)S(1)}, u32[]{:S(2)}, u32[]{:S(2)}) %collective-permute-start.20) | collective-permute-done | bytes 409632 | tf_op jit(solution)/shard_map/ppermute | solution.py:209
  425.7 15.8 %conditional.15 = ((bf16[160,1280]{1,0:T(8,128)(2,1)}, bf16[160,1280]{1,0:T(8,128)(2,1)})) conditional(s32[]{:T(128)} %convert_element_type.128, (bf16[160,1280]{1,0:T(8,128)(2,1)}, bf16[160,1280]{1,0:T(8,128)(2,1)}) %tuple.92, (bf16[160,1280]{1,0:T(8,128)(2,1)S(1)}, bf16[160,1280]{1,0:T(8,128)(2,1)}, bf16[160,1280]{1,0:T(8,128)(2,1)}, ...), branch_computations={%region_34.35_spmd, %region_35.39_spmd} | conditional | flops 1051689088 | bytes 18110812 | solution.py:337
  425.7 9.9 %branch_1_fun.27 = (f32[160,1408]{1,0:T(8,128)}, f32[160,1280]{1,0:T(8,128)}) custom-call(s32[1]{0:T(128)} %get-tuple-element.192.core_ref, bf16[160,1280]{1,0:T(8,128)(2,1)S(1)} %get-tuple-element.363.grad_ref, bf16[160,1280]{1,0:T(8,128)(2,1)} %get-tuple-element.190.own_ref, bf16[160,1280]{1,0:T(8,128)(2,1)} %get-tuple-element.191.other_ref, ...), custom_call_target="tpu_custom_call" | custom-call | flops 1048576000 | bytes 6553600 | tf_op jit(solution)/shard_map/cond/branch_1_fun/pallas_call | solution.py:108
  439.3 2.1 fusion.47
  442.8 1.6 collective-permute-done.21
  446.5 34.4 %all_to_all.70 = bf16[160,8,320]{2,0,1:T(8,128)(2,1)S(1)} all-to-all(bf16[160,8,320]{2,0,1:T(8,128)(2,1)S(1)} %copy.26), channel_id=1, replica_groups={{0,4,8,12,16,20,24,28},{1,5,9,13,17,21,25,29},{2,6,10,14,18,22,26,30},{..., dimensions={1} | all-to-all | bytes 1638400 | tf_op jit(solution)/shard_map/all_to_all | solution.py:228
  482.2 16.1 %all-gather.2 = f32[8,160,160]{2,1,0:T(8,128)} all-gather(f32[2,160,160]{2,1,0:T(8,128)S(1)} %pad_maximum_fusion.5), channel_id=4, replica_groups={{0,1,2,3},{4,5,6,7},{8,9,10,11},{12,13,14,15},{16,17,18,19},{20,21,22,2..., dimensions={0}, use_global_device_ids=true | all-gather | bytes 1024000 | tf_op jit(solution)/shard_map/all_gather | solution.py:250
  498.3 18.2 %shard_map.62 = bf16[2,160,160]{2,1,0:T(8,128)(2,1)} custom-call(f32[4,2,160,160]{3,2,1,0:T(8,128)} %bitcast.44, f32[1]{0:T(128)} %bitcast.9.count_ref), custom_call_target="tpu_custom_call" | custom-call | tf_op jit(solution)/shard_map/pallas_call | solution.py:190
  519.9 26.8 %all_to_all.71 = bf16[8,160,320]{2,1,0:T(8,128)(2,1)S(1)} all-to-all(bf16[8,160,320]{2,1,0:T(8,128)(2,1)S(1)} %bitcast.45), channel_id=1, replica_groups={{0,4,8,12,16,20,24,28},{1,5,9,13,17,21,25,29},{2,6,10,14,18,22,26,30},{..., dimensions={0} | all-to-all | bytes 1638400 | tf_op jit(solution)/shard_map/all_to_all | solution.py:235
  547.1 1.5 broadcast_in_dim.59
  (95 shorter events, 36.8 us)
Async XLA Ops:
  7.2 128.0 %copy-start.7 = (bf16[160,2560]{1,0:T(8,128)(2,1)S(1)}, bf16[160,2560]{1,0:T(8,128)(2,1)}, u32[]{:S(2)}) copy-start(bf16[160,2560]{1,0:T(8,128)(2,1)} %param.20) | copy-start | bytes 2457604
  7.2 128.0 %all-gather.5.cloned.1.call-start = ((), (), s32[]{:S(2)}) async-start(), calls=%async_computation.4 | async-start | bytes 13516800 | tf_op jit(solution)/shard_map/all_gather | solution.py:278
  8.4 1.5 collective-permute-start.14
  136.0 6.4 %copy-start = (bf16[160,1280]{1,0:T(8,128)(2,1)}, bf16[160,1280]{1,0:T(8,128)(2,1)S(1)}, u32[]{:S(2)}) copy-start(bf16[160,1280]{1,0:T(8,128)(2,1)S(1)} %get-tuple-element.309.own_ref) | copy-start | bytes 1228804 | tf_op jit(solution)/shard_map/cond
  142.4 2.1 collective-permute-start.6
  142.4 7.8 %copy-start.1 = (bf16[160,1280]{1,0:T(8,128)(2,1)S(1)}, bf16[160,1280]{1,0:T(8,128)(2,1)}, u32[]{:S(2)}) copy-start(bf16[160,1280]{1,0:T(8,128)(2,1)} %copy-done) | copy-start | bytes 1228804 | tf_op jit(solution)/shard_map/cond
  150.2 10.6 %collective-permute-start.15 = (bf16[160,1280]{1,0:T(8,128)(2,1)S(1)}, bf16[160,1280]{1,0:T(8,128)(2,1)S(1)}, u32[]{:S(2)}, u32[]{:S(2)}) collective-permute-start(bf16[160,1280]{1,0:T(8,128)(2,1)S(1)} %get-tuple-element.241), channel_id=1, source_target_pairs={{0,64},{32,96},{1,65},{33,97},{2,66},{34,98},{3,67},{35,99},{4,68}... | collective-permute-start | bytes 1228808 | tf_op jit(solution)/shard_map/ppermute | solution.py:209
  160.9 0.7 collective-permute-start.16
  161.6 0.7 collective-permute-start.17
  162.4 1.3 copy-start.3
  167.0 5.7 %copy-start.9 = (u32[256]{0:T(256)S(1)}, u32[256]{0:T(256)}, u32[]{:S(2)}) copy-start(u32[256]{0:T(256)} %constant.117) | copy-start | bytes 3076
  167.1 6.9 %copy-start.8 = (s32[5]{0:T(128)S(1)}, s32[5]{0:T(128)}, u32[]{:S(2)}) copy-start(s32[5]{0:T(128)} %param.23) | copy-start | bytes 64
  168.4 37.5 %all-to-all-start = ((bf16[160,8,320]{2,0,1:T(8,128)(2,1)}), bf16[160,8,320]{2,0,1:T(8,128)(2,1)S(1)}, u32[]{:S(2)}, u32[]{:S(2)}) async-start(bf16[160,8,320]{2,0,1:T(8,128)(2,1)} %multiply_convert_fusion), calls=%async_computation | async-start | bytes 1966080 | tf_op jit(solution)/shard_map/all_to_all | solution.py:228
  205.2 18.4 %collective-permute-start.18 = (bf16[160,1280]{1,0:T(8,128)(2,1)S(1)}, bf16[160,1280]{1,0:T(8,128)(2,1)S(1)}, u32[]{:S(2)}, u32[]{:S(2)}) collective-permute-start(bf16[160,1280]{1,0:T(8,128)(2,1)S(1)} %get-tuple-element.258), channel_id=1, source_target_pairs={{192,128},{224,160},{193,129},{225,161},{194,130},{226,162},{195,1... | collective-permute-start | bytes 1228808 | tf_op jit(solution)/shard_map/ppermute | solution.py:209
  246.3 29.2 %all-to-all-start.1 = ((bf16[8,160,320]{2,1,0:T(8,128)(2,1)}), bf16[8,160,320]{2,1,0:T(8,128)(2,1)S(1)}, u32[]{:S(2)}, u32[]{:S(2)}) async-start(bf16[8,160,320]{2,1,0:T(8,128)(2,1)} %bitcast.12), calls=%async_computation.1 | async-start | bytes 1966080 | tf_op jit(solution)/shard_map/all_to_all | solution.py:235
  250.8 26.5 %collective-permute-start.19 = (bf16[160,1280]{1,0:T(8,128)(2,1)S(1)}, bf16[160,1280]{1,0:T(8,128)(2,1)S(1)}, u32[]{:S(2)}, u32[]{:S(2)}) collective-permute-start(bf16[160,1280]{1,0:T(8,128)(2,1)S(1)} %get-tuple-element.262), channel_id=1, source_target_pairs={{128,64},{160,96},{129,65},{161,97},{130,66},{162,98},{131,67},{16... | collective-permute-start | bytes 1228808 | tf_op jit(solution)/shard_map/ppermute | solution.py:209
  277.4 148.3 %collective-permute-start.20 = (bf16[160,1280]{1,0:T(8,128)(2,1)S(1)}, bf16[160,1280]{1,0:T(8,128)(2,1)S(1)}, u32[]{:S(2)}, u32[]{:S(2)}) collective-permute-start(bf16[160,1280]{1,0:T(8,128)(2,1)S(1)} %get-tuple-element.273), channel_id=1, source_target_pairs={{64,0},{96,32},{65,1},{97,33},{66,2},{98,34},{67,3},{99,35},{68,4}... | collective-permute-start | bytes 1228808 | tf_op jit(solution)/shard_map/ppermute | solution.py:209
  435.6 3.7 copy-start.4
  435.6 2.7 collective-permute-start.13
  442.6 1.8 collective-permute-start.21
Sparse Core Ops, SparseCore 0:
  11.9 123.2 all-gather.4

commit v2 on v1

--- a/solution.py
+++ b/solution.py
@@ -1,3 +1,5 @@
+import functools
+
 import jax
 import jax.numpy as jnp
 from jax import lax
@@ -5,11 +7,13 @@
 from jax.experimental.pallas import tpu as pltpu
 from jax.sharding import PartitionSpec as P
 
+
 BLOCK = 160
 EPSILON = 1e-05
 DAMPING = 0.1
 LANES = 128
-TILE = 256
+TILE = 640
+ROWS = 640
 
 f32 = jnp.float32
 bf16 = jnp.bfloat16
@@ -64,17 +68,55 @@
     )(core, own, other, weight, weight)
 
 
-def backward_kernel(core_ref, grad_ref, own_ref, other_ref, weight_ref, send_ref, keep_ref, factor):
+def finish(grad, keep, sent, arrived, own):
+    half = own.shape[1]
+    mean = jnp.sum(sent + arrived[:, half:], axis=-1, keepdims=True) / (2 * half)
+    factor = keep[:, half : half + 1]
+    back = keep[:, :half] + arrived[:, :half]
+    through = factor * (back - own.astype(f32) * factor * mean)
+    return (grad.astype(f32) + through).astype(bf16)
+
+
+def finish_kernel(grad_ref, keep_ref, sent_ref, arrived_ref, own_ref, out_ref):
+    out_ref[...] = finish(
+        grad_ref[...], keep_ref[...], sent_ref[...], arrived_ref[...], own_ref[...]
+    )
+
+
+def finish_layer(grad, keep, send, arrived, own):
+    rows, half = own.shape
+    whole = pl.BlockSpec((rows, half), lambda i: (0, 0))
+    wide = pl.BlockSpec((rows, half + LANES), lambda i: (0, 0))
+    return pl.pallas_call(
+        finish_kernel,
+        out_shape=jax.ShapeDtypeStruct((rows, half), bf16),
+        grid=(1,),
+        in_specs=[whole, wide, pl.BlockSpec((rows, LANES), lambda i: (0, half // LANES)), wide, whole],
+        out_specs=whole,
+        cost_estimate=pl.CostEstimate(
+            flops=8 * rows * half, bytes_accessed=16 * rows * half, transcendentals=0
+        ),
+    )(grad, keep, send, arrived, own)
+
+
+def backward_kernel(fused, core_ref, *refs):
+    if fused:
+        before, refs = refs[:5], refs[5:]
+        own_ref, other_ref, weight_ref, send_ref, keep_ref, grad_ref = refs
+    else:
+        grad_ref, own_ref, other_ref, weight_ref, send_ref, keep_ref = refs
     step = pl.program_id(0)
-    half = own_ref.shape[1]
-    steps = half // TILE
+    rows, half = own_ref.shape
+    steps = half // ROWS
 
     @pl.when(step == 0)
     def _():
+        if fused:
+            grad_ref[...] = finish(*[ref[...] for ref in before])
         own = own_ref[...].astype(f32)
         other = other_ref[...].astype(f32)
-        factor[...] = jnp.broadcast_to(row_factor(own, other, 2 * half), factor.shape)
-        send_ref[:, half:] = jnp.zeros((own.shape[0], LANES), f32)
+        keep_ref[:, half:] = jnp.broadcast_to(row_factor(own, other, 2 * half), (rows, LANES))
+        send_ref[:, half:] = jnp.zeros((rows, LANES), f32)
 
     part = lax.dot_general(
         grad_ref[...], weight_ref[...], (((1,), (1,)), ((), ())), preferred_element_type=f32
@@ -82,54 +124,53 @@
 
     def along(hidden_ref, columns):
         product = part * hidden_ref[:, columns].astype(f32)
-        send_ref[:, half:] += (product[:, :LANES] + product[:, LANES:]) * factor[...]
+        folded = product[:, :LANES]
+        for k in range(1, ROWS // LANES):
+            folded = folded + product[:, k * LANES : (k + 1) * LANES]
+        send_ref[:, half:] += folded * keep_ref[:, half:]
 
     @pl.when(step < steps)
     def _():
-        columns = pl.ds(pl.multiple_of(step * TILE, TILE), TILE)
+        columns = pl.ds(pl.multiple_of(step * ROWS, LANES), ROWS)
+        send_ref[:, columns] = part
         along(other_ref, columns)
-        send_ref[:, columns] = part
 
     @pl.when(step >= steps)
     def _():
-        columns = pl.ds(pl.multiple_of((step - steps) * TILE, TILE), TILE)
+        columns = pl.ds(pl.multiple_of((step - steps) * ROWS, LANES), ROWS)
+        keep_ref[:, columns] = part
         along(own_ref, columns)
-        keep_ref[:, columns] = part
-
-
-def backward_layer(core, grad, own, other, weight, which):
+
+
+def backward_layer(core, before, own, other, weight, which):
     rows, half = own.shape
-    steps = half // TILE
+    steps = half // ROWS
+    fused = len(before) > 1
     whole = pl.BlockSpec((rows, half), lambda i, c: (0, 0))
+    wide = pl.BlockSpec((rows, half + LANES), lambda i, c: (0, 0))
+    tail = pl.BlockSpec((rows, LANES), lambda i, c: (0, half // LANES))
 
     def place(i, c):
         return (jnp.where(i < steps, (1 - c[0]) * steps + i, c[0] * steps + i - steps), which)
 
-    send, keep = pl.pallas_call(
-        backward_kernel,
-        out_shape=[
-            jax.ShapeDtypeStruct((rows, half + LANES), f32),
-            jax.ShapeDtypeStruct((rows, half), f32),
-        ],
+    out_shape = [jax.ShapeDtypeStruct((rows, half + LANES), f32)] * 2
+    first = [whole, wide, tail, wide, whole] if fused else [whole]
+    results = pl.pallas_call(
+        functools.partial(backward_kernel, fused),
+        out_shape=out_shape + [jax.ShapeDtypeStruct((rows, half), bf16)] * fused,
         grid_spec=pltpu.PrefetchScalarGridSpec(
             num_scalar_prefetch=1,
             grid=(2 * steps,),
-            in_specs=[whole, whole, whole, pl.BlockSpec((TILE, half), place)],
-            out_specs=[pl.BlockSpec((rows, half + LANES), lambda i, c: (0, 0)), whole],
-            scratch_shapes=[pltpu.VMEM((rows, LANES), f32)],
+            in_specs=first + [whole, whole, pl.BlockSpec((ROWS, half), place)],
+            out_specs=[wide, wide] + [whole] * fused,
         ),
         cost_estimate=pl.CostEstimate(
             flops=4 * rows * half * half, bytes_accessed=4 * half * half, transcendentals=0
         ),
-    )(core, grad, own, other, weight)
-    arrived = swap_cores(send)
-    width = 2 * half
-    wide_own, wide_other = own.astype(f32), other.astype(f32)
-    factor = row_factor(wide_own, wide_other, width)
-    mean = jnp.sum(send[:, half:] + arrived[:, half:], axis=-1, keepdims=True) / width
-    back = keep + arrived[:, :half]
-    through = factor * (back - wide_own * factor * mean)
-    return (grad.astype(f32) + through).astype(bf16)
+    )(core, *before, own, other, weight)
+    send, keep = results[:2]
+    grad = results[2] if fused else before[0]
+    return (grad, keep, send, swap_cores(send), own)
 
 
 PANEL = 32
@@ -162,7 +203,7 @@
         inside_row = (rows >= start) & (rows < stop)
         inside_column = (columns >= start) & (columns < stop)
         strip_column = inside_column[:PANEL]
-        unit = small_rows_eye(small_rows, columns[:PANEL], start)
+        unit = small_rows_eye(columns[:PANEL], start)
         for m in range(many):
             strip = jnp.where(strip_column, unit, strips[m])
             solved = jnp.dot(
@@ -180,7 +221,7 @@
         out_ref[m] = (-work[m]).astype(bf16)
 
 
-def small_rows_eye(small_rows, wide_columns, start):
+def small_rows_eye(wide_columns, start):
     rows = lax.broadcasted_iota(jnp.int32, wide_columns.shape, 0)
     return jnp.where(wide_columns == rows + start, -1.0, 0.0)
 
@@ -261,7 +302,7 @@
     return jnp.concatenate(results, axis=1)
 
 
-def on_device(inputs, cotangent, weights, lengths):
+def all_stages(inputs, cotangent, weights, lengths):
     section = lax.axis_index("section")
     chip, core = section // 2, section % 2
     chips = lax.axis_size("section") // 2
@@ -291,6 +332,7 @@
         return jnp.where(core == 0, array[:, half:], array[:, :half])
 
     first_own = own_half(inputs)
+    first_own, counted, live = lax.optimization_barrier((first_own, counted, live))
     empty = jnp.zeros((tokens, half), bf16)
     kept = (empty, empty, empty, empty)
     arriving = first_own
@@ -324,12 +366,11 @@
 
         def turn(operands, stage=stage):
             grad, own_a, other_a, own_b, other_b, weight = operands
-            grad_a = backward_layer(scalar_core, grad, own_b, other_b, weight, 1)
+            pieces = backward_layer(scalar_core, (grad,), own_b, other_b, weight, 1)
             if stage == 0:
-                leaving = empty
-            else:
-                leaving = backward_layer(scalar_core, grad_a, own_a, other_a, weight, 0)
-            return (grad_a, grad), leaving
+                return (finish_layer(*pieces), grad), empty
+            pieces = backward_layer(scalar_core, pieces, own_a, other_a, weight, 0)
+            return (pieces[0], grad), finish_layer(*pieces)
 
         def rest(operands, grads=grads):
             return grads, empty
@@ -345,7 +386,8 @@
             own, other, leaving = lax.optimization_barrier((own, other, leaving))
             full = halves(core, own, other).astype(f32)
             mean = jnp.mean(full * full, axis=-1, keepdims=True)
-            taken = spread((full * lax.rsqrt(mean + EPSILON)).astype(bf16))
+            full = (full * lax.rsqrt(mean + EPSILON)).astype(bf16)
+            taken = spread(full)
             parts = gram_parts(taken, live)
             arriving, parts = lax.optimization_barrier((arriving, parts))
         elif stage == chips - 2:
@@ -367,5 +409,5 @@
     in_specs = (P("dp", None), P("dp", None), P("section", "dp", None), P("dp"))
     out_specs = (P("section", "dp", None), P("section", "dp", None))
     return jax.shard_map(
-        on_device, mesh=mesh, in_specs=in_specs, out_specs=out_specs, check_vma=False
+        all_stages, mesh=mesh, in_specs=in_specs, out_specs=out_specs, check_vma=False
     )

time: 566 us -> 502 us (0.89)
  waiting for transfers between devices: 309 us -> 260 us
  blocking collectives: 123 us -> 116 us
    ppermute x6, waiting for transfers between devices: 156 us -> 104 us  [hop(): return lax.ppermute(array, 'section', pairs)]
    all_to_all x1, waiting for transfers between devices: 0.01 us -> 26.5 us  [spread(): lax.all_to_all(values, 'dp', split_axis=1, concat_axis=0, axis_index_grou...]
    all_gather x1, waiting for transfers between devices: 123 us -> 97.6 us  [all_stages(): weight = lax.all_gather(paired, 'dp', axis=0, tiled=True)]
    unnamed x1, blocking collectives: 29.3 us -> 22.6 us
  transfers between devices with their start and end apart: 13 -> 13, of which waited for: 8 -> 9; matrix products, arithmetic and copies ran while one was open for 1% -> 1% of each run, Pallas kernels for 0% -> 0%
where the time goes in v2:
time: 502 us; the launch traced here: 493 us
  waiting for transfers between devices  260 us (52%)
  blocking collectives  116 us (23%)
  Pallas kernels  54.8 us (11%)
  between operations  16.2 us (3%)
  starting transfers between devices  13.6 us (3%)
  local copies, waits for them, and re-layouts  13.2 us (3%)
  other arithmetic  10.2 us (2%)
  matrix products  7.57 us (2%)
    ppermute x6, waiting for transfers between devices, hop(): return lax.ppermute(array, 'section', pairs)  104 us
    all_gather x1, waiting for transfers between devices, all_stages(): weight = lax.all_gather(paired, 'dp', axis=0, tiled=True)  97.6 us
    pallas_call x2, Pallas kernels, invert_blocks(): pl.pallas_call(inverse_kernel, out_shape=jax.ShapeDtypeStruct((many, orde...  36.4 us
    all_to_all x1, blocking collectives, spread(): lax.all_to_all(values, 'dp', split_axis=1, concat_axis=0, axis_index_grou...  34.4 us
    all_gather x2, blocking collectives, gram_parts(): lax.all_gather(jnp.stack(grams), 'dp', axis=0, axis_index_groups=mates)  32.7 us
    all_to_all x1, blocking collectives, gather_back(): lax.all_to_all(values, 'dp', split_axis=0, concat_axis=1, axis_index_grou...  26.8 us
    all_to_all x1, waiting for transfers between devices, spread(): lax.all_to_all(values, 'dp', split_axis=1, concat_axis=0, axis_index_grou...  26.5 us
    all_to_all x1, waiting for transfers between devices, gather_back(): lax.all_to_all(values, 'dp', split_axis=0, concat_axis=1, axis_index_grou...  25 us
  transfers between devices with their start and end apart: 13, of which 9 were waited for; matrix products, arithmetic and copies ran while one was open for 1% of the time, Pallas kernels for 0%

profile of v2, /device:TPU:2, one launch (start us, length us, event | category | flops | bytes accessed | tf_op | source)
XLA Modules:
  0.0 492.5 jit_solution(1626470456038436085)
XLA Ops:
  13.4 22.6 %all-reduce = s32[160]{0:T(256)S(1)} all-reduce(s32[160]{0:T(256)S(1)} %dynamic-update-slice), channel_id=2, replica_groups=mesh['section'=8,'dp'=32] {'dp'}, use_global_device_ids=true, to_apply=%add | all-reduce | flops 160 | bytes 1280
  37.7 97.6 %all-gather.5.cloned.1.call-done = bf16[2560,2560]{1,0:T(8,128)(2,1)} async-done(((bf16[80,2560]{1,0:T(8,128)(2,1)}), bf16[2560,2560]{1,0:T(8,128)(2,1)}) %all-gather.5.cloned.1.call-update) | async-done | bytes 13107216 | tf_op jit(solution)/shard_map/all_gather | solution.py:319
  135.3 11.7 %conditional.8 = (bf16[160,1280]{1,0:T(8,128)(2,1)S(1)}, bf16[160,1280]{1,0:T(8,128)(2,1)}, bf16[160,1280]{1,0:T(8,128)(2,1)}, bf16[160,1280]{1,0:T(8,128)(2,1)}, bf16[160,1280]{1,0:T(8,128)(2,1)S(1)}) conditional(s32[]{:T(128)} %convert_element_type.44, () %tuple.76, (s32[]{:T(128)}, bf16[160,2560]{1,0:T(8,128)(2,1)S(1)}, s32[1]{0:T(128)}, ...), branch_computations={%region_1.2_spmd, %region_2.3_spmd} | conditional | flops 2097356800 | bytes 15974490 | solution.py:356
  136.1 4.7 branch_1_fun.18.own_ref
  140.8 2.1 collective-permute-done.11.other_ref
  142.8 4.1 branch_1_fun.19
  148.3 9.3 %collective-permute-done.15 = bf16[160,1280]{1,0:T(8,128)(2,1)S(1)} collective-permute-done((bf16[160,1280]{1,0:T(8,128)(2,1)S(1)}, bf16[160,1280]{1,0:T(8,128)(2,1)S(1)}, u32[]{:S(2)}, u32[]{:S(2)}) %collective-permute-start.15) | collective-permute-done | bytes 409632 | tf_op jit(solution)/shard_map/ppermute | solution.py:250
  160.7 2.4 conditional.12
  166.0 4.4 all-to-all-start
  171.0 26.5 %all-to-all-done = bf16[160,8,320]{2,0,1:T(8,128)(2,1)S(1)} async-done(((bf16[160,8,320]{2,0,1:T(8,128)(2,1)}), bf16[160,8,320]{2,0,1:T(8,128)(2,1)S(1)}, u32[]{:S(2)}, u32[]{:S(2)}) %all-to-all-start) | async-done | bytes 819232 | tf_op jit(solution)/shard_map/all_to_all | solution.py:269
  198.9 16.6 %all-gather.1 = f32[8,160,160]{2,1,0:T(8,128)} all-gather(f32[2,160,160]{2,1,0:T(8,128)S(1)} %pad_maximum_fusion.4), channel_id=3, replica_groups={{0,1,2,3},{4,5,6,7},{8,9,10,11},{12,13,14,15},{16,17,18,19},{20,21,22,2..., dimensions={0}, use_global_device_ids=true | all-gather | bytes 1024000 | tf_op jit(solution)/shard_map/all_gather | solution.py:291
  215.7 18.2 %shard_map.60 = bf16[2,160,160]{2,1,0:T(8,128)(2,1)} custom-call(f32[4,2,160,160]{3,2,1,0:T(8,128)} %bitcast.43, f32[1]{0:T(128)} %bitcast.2.count_ref), custom_call_target="tpu_custom_call" | custom-call | tf_op jit(solution)/shard_map/pallas_call | solution.py:231
  238.0 3.6 all-to-all-start.1
  242.3 25.0 %all-to-all-done.1 = bf16[8,160,320]{2,1,0:T(8,128)(2,1)S(1)} async-done(((bf16[8,160,320]{2,1,0:T(8,128)(2,1)}), bf16[8,160,320]{2,1,0:T(8,128)(2,1)S(1)}, u32[]{:S(2)}, u32[]{:S(2)}) %all-to-all-start.1) | async-done | bytes 819232 | tf_op jit(solution)/shard_map/all_to_all | solution.py:276
  270.5 94.3 %collective-permute-done.20 = bf16[160,1280]{1,0:T(8,128)(2,1)S(1)} collective-permute-done((bf16[160,1280]{1,0:T(8,128)(2,1)S(1)}, bf16[160,1280]{1,0:T(8,128)(2,1)S(1)}, u32[]{:S(2)}, u32[]{:S(2)}) %collective-permute-start.20) | collective-permute-done | bytes 409632 | tf_op jit(solution)/shard_map/ppermute | solution.py:250
  364.8 13.5 %conditional.15 = ((bf16[160,1280]{1,0:T(8,128)(2,1)}, bf16[160,1280]{1,0:T(8,128)(2,1)})) conditional(s32[]{:T(128)} %convert_element_type.44, (bf16[160,1280]{1,0:T(8,128)(2,1)}, bf16[160,1280]{1,0:T(8,128)(2,1)}) %tuple.94, (s32[1]{0:T(128)}, bf16[160,1280]{1,0:T(8,128)(2,1)S(1)}, bf16[160,1280]{1,0:T(8,128)(2,1)}, ...), branch_computations={%region_16.17_spmd, %region_17.18_spmd} | conditional | flops 1050214400 | bytes 17858652 | solution.py:378
  364.8 7.0 %branch_1_fun.34 = (f32[160,1408]{1,0:T(8,128)}, f32[160,1408]{1,0:T(8,128)}) custom-call(s32[1]{0:T(128)} %get-tuple-element.187.core_ref, bf16[160,1280]{1,0:T(8,128)(2,1)S(1)} %get-tuple-element.348.refs_0_.grad_ref, bf16[160,1280]{1,0:T(8,128)(2,1)} %get-tuple-element.188.refs_1_.own_ref, bf16[160,1280]{1,0:T(8,128)(2,1)} %get-tuple-element.189.refs_2_, ...), custom_call_target="tpu_custom_call" | custom-call | flops 1048576000 | bytes 6553600 | tf_op jit(solution)/shard_map/cond/branch_1_fun/pallas_call | solution.py:158
  372.5 1.9 collective-permute-done.10.arrived_ref
  375.3 2.7 branch_1_fun.35
  379.5 1.6 collective-permute-done.21
  383.1 34.4 %all_to_all.70 = bf16[160,8,320]{2,0,1:T(8,128)(2,1)S(1)} all-to-all(bf16[160,8,320]{2,0,1:T(8,128)(2,1)S(1)} %copy.25), channel_id=1, replica_groups={{0,4,8,12,16,20,24,28},{1,5,9,13,17,21,25,29},{2,6,10,14,18,22,26,30},{..., dimensions={1} | all-to-all | bytes 1638400 | tf_op jit(solution)/shard_map/all_to_all | solution.py:269
  418.9 16.1 %all-gather.2 = f32[8,160,160]{2,1,0:T(8,128)} all-gather(f32[2,160,160]{2,1,0:T(8,128)S(1)} %pad_maximum_fusion.5), channel_id=4, replica_groups={{0,1,2,3},{4,5,6,7},{8,9,10,11},{12,13,14,15},{16,17,18,19},{20,21,22,2..., dimensions={0}, use_global_device_ids=true | all-gather | bytes 1024000 | tf_op jit(solution)/shard_map/all_gather | solution.py:291
  435.0 18.2 %shard_map.61 = bf16[2,160,160]{2,1,0:T(8,128)(2,1)} custom-call(f32[4,2,160,160]{3,2,1,0:T(8,128)} %bitcast.44, f32[1]{0:T(128)} %bitcast.2.count_ref), custom_call_target="tpu_custom_call" | custom-call | tf_op jit(solution)/shard_map/pallas_call | solution.py:231
  456.6 26.8 %all_to_all.71 = bf16[8,160,320]{2,1,0:T(8,128)(2,1)S(1)} all-to-all(bf16[8,160,320]{2,1,0:T(8,128)(2,1)S(1)} %bitcast.45), channel_id=1, replica_groups={{0,4,8,12,16,20,24,28},{1,5,9,13,17,21,25,29},{2,6,10,14,18,22,26,30},{..., dimensions={0} | all-to-all | bytes 1638400 | tf_op jit(solution)/shard_map/all_to_all | solution.py:276
  (89 shorter events, 38.8 us)
Async XLA Ops:
  7.2 4.7 copy-start.11
  7.2 5.9 %copy-start.10 = (s32[5]{0:T(128)S(1)}, s32[5]{0:T(128)}, u32[]{:S(2)}) copy-start(s32[5]{0:T(128)} %param.23) | copy-start | bytes 64
  7.2 30.4 %copy-start.1 = (bf16[160,2560]{1,0:T(8,128)(2,1)S(1)}, bf16[160,2560]{1,0:T(8,128)(2,1)}, u32[]{:S(2)}) copy-start(bf16[160,2560]{1,0:T(8,128)(2,1)} %param.20) | copy-start | bytes 2457604
  7.2 128.1 %all-gather.5.cloned.1.call-start = ((), (), s32[]{:S(2)}) async-start(), calls=%async_computation.4 | async-start | bytes 13516800 | tf_op jit(solution)/shard_map/all_gather | solution.py:319
  8.4 1.5 collective-permute-start.14
  140.8 2.1 collective-permute-start.11
  147.0 10.6 %collective-permute-start.15 = (bf16[160,1280]{1,0:T(8,128)(2,1)S(1)}, bf16[160,1280]{1,0:T(8,128)(2,1)S(1)}, u32[]{:S(2)}, u32[]{:S(2)}) collective-permute-start(bf16[160,1280]{1,0:T(8,128)(2,1)S(1)} %get-tuple-element.242), channel_id=1, source_target_pairs={{0,64},{32,96},{1,65},{33,97},{2,66},{34,98},{3,67},{35,99},{4,68}... | collective-permute-start | bytes 1228808 | tf_op jit(solution)/shard_map/ppermute | solution.py:250
  157.6 0.7 collective-permute-start.16
  158.4 0.7 collective-permute-start.17
  159.5 1.3 copy-start.9
  166.0 31.5 %all-to-all-start = ((bf16[160,8,320]{2,0,1:T(8,128)(2,1)}), bf16[160,8,320]{2,0,1:T(8,128)(2,1)S(1)}, u32[]{:S(2)}, u32[]{:S(2)}) async-start(bf16[160,8,320]{2,0,1:T(8,128)(2,1)} %multiply_convert_fusion), calls=%async_computation | async-start | bytes 1966080 | tf_op jit(solution)/shard_map/all_to_all | solution.py:269
  170.4 45.1 %collective-permute-start.18 = (bf16[160,1280]{1,0:T(8,128)(2,1)}, bf16[160,1280]{1,0:T(8,128)(2,1)S(1)}, u32[]{:S(2)}, u32[]{:S(2)}) collective-permute-start(bf16[160,1280]{1,0:T(8,128)(2,1)} %get-tuple-element.259), channel_id=1, source_target_pairs={{192,128},{224,160},{193,129},{225,161},{194,130},{226,162},{195,1... | collective-permute-start | bytes 1228808 | tf_op jit(solution)/shard_map/ppermute | solution.py:250
  238.0 29.3 %all-to-all-start.1 = ((bf16[8,160,320]{2,1,0:T(8,128)(2,1)}), bf16[8,160,320]{2,1,0:T(8,128)(2,1)S(1)}, u32[]{:S(2)}, u32[]{:S(2)}) async-start(bf16[8,160,320]{2,1,0:T(8,128)(2,1)} %bitcast.12), calls=%async_computation.1 | async-start | bytes 1966080 | tf_op jit(solution)/shard_map/all_to_all | solution.py:276
  241.6 27.6 %collective-permute-start.19 = (bf16[160,1280]{1,0:T(8,128)(2,1)S(1)}, bf16[160,1280]{1,0:T(8,128)(2,1)S(1)}, u32[]{:S(2)}, u32[]{:S(2)}) collective-permute-start(bf16[160,1280]{1,0:T(8,128)(2,1)S(1)} %get-tuple-element.264), channel_id=1, source_target_pairs={{128,64},{160,96},{129,65},{161,97},{130,66},{162,98},{131,67},{16... | collective-permute-start | bytes 1228808 | tf_op jit(solution)/shard_map/ppermute | solution.py:250
  269.2 95.6 %collective-permute-start.20 = (bf16[160,1280]{1,0:T(8,128)(2,1)S(1)}, bf16[160,1280]{1,0:T(8,128)(2,1)S(1)}, u32[]{:S(2)}, u32[]{:S(2)}) collective-permute-start(bf16[160,1280]{1,0:T(8,128)(2,1)S(1)} %get-tuple-element.276), channel_id=1, source_target_pairs={{64,0},{96,32},{65,1},{97,33},{66,2},{98,34},{67,3},{99,35},{68,4}... | collective-permute-start | bytes 1228808 | tf_op jit(solution)/shard_map/ppermute | solution.py:250
  371.7 2.7 collective-permute-start.10
  374.4 0.9 copy-start.2
  379.3 1.8 collective-permute-start.21
Sparse Core Ops, SparseCore 0:
  11.9 123.3 all-gather.4

commit v3 on v2

--- a/solution.py
+++ b/solution.py
@@ -173,71 +173,40 @@
     return (grad, keep, send, swap_cores(send), own)
 
 
-PANEL = 32
-
-
-def inverse_kernel(gram_ref, count_ref, out_ref, work):
-    many, order = work.shape[0], work.shape[1]
-    counted = count_ref[0]
+def inverse_kernel(first_ref, second_ref, count_ref, out_ref):
+    order = out_ref.shape[0]
     rows = lax.broadcasted_iota(jnp.int32, (order, order), 0)
     columns = lax.broadcasted_iota(jnp.int32, (order, order), 1)
-    small_rows = lax.broadcasted_iota(jnp.int32, (PANEL, PANEL), 0)
-    small_columns = lax.broadcasted_iota(jnp.int32, (PANEL, PANEL), 1)
-    for m in range(many):
-        total = gram_ref[0, m]
-        for part in range(1, gram_ref.shape[0]):
-            total = total + gram_ref[part, m]
-        work[m] = total / counted + jnp.where(rows == columns, DAMPING, 0.0)
-    for start in range(0, order, PANEL):
-        stop = start + PANEL
-        strips = [work[m, start:stop, :] for m in range(many)]
-        pivots = [strip[:, start:stop] for strip in strips]
-        for k in range(PANEL):
-            keep = (small_rows != k) & (small_columns != k)
-            for m in range(many):
-                block = pivots[m]
-                pivot = block[k : k + 1, k : k + 1]
-                row = jnp.where(small_columns[:1] == k, -1.0, block[k : k + 1, :])
-                column = jnp.where(small_rows[:, :1] == k, -1.0, block[:, k : k + 1])
-                pivots[m] = jnp.where(keep, block, 0.0) - column * (row / pivot)
-        inside_row = (rows >= start) & (rows < stop)
-        inside_column = (columns >= start) & (columns < stop)
-        strip_column = inside_column[:PANEL]
-        unit = small_rows_eye(columns[:PANEL], start)
-        for m in range(many):
-            strip = jnp.where(strip_column, unit, strips[m])
-            solved = jnp.dot(
-                -pivots[m], strip, precision=lax.Precision.HIGHEST, preferred_element_type=f32
-            )
-            change = lax.dot_general(
-                strip,
-                solved,
-                (((0,), (0,)), ((), ())),
-                precision=lax.Precision.HIGHEST,
-                preferred_element_type=f32,
-            )
-            work[m] = jnp.where(inside_row | inside_column, 0.0, work[m]) - change
-    for m in range(many):
-        out_ref[m] = (-work[m]).astype(bf16)
-
-
-def small_rows_eye(wide_columns, start):
-    rows = lax.broadcasted_iota(jnp.int32, wide_columns.shape, 0)
-    return jnp.where(wide_columns == rows + start, -1.0, 0.0)
-
-
-def invert_blocks(parts, counted):
-    many, order = parts.shape[1], parts.shape[2]
+    row, column = columns[:1], rows[:, :1]
+    block = (first_ref[...] + second_ref[...]) / count_ref[0]
+    block = block + jnp.where(rows == columns, DAMPING, 0.0)
+    for k in range(0, order, 2):
+        n = k + 1
+        a, b, c = block[k : k + 1, k : k + 1], block[k : k + 1, n : n + 1], block[n : n + 1, n : n + 1]
+        scale = 1.0 / (a * c - b * b)
+        row_k = jnp.where(row == k, -1.0, jnp.where(row == n, 0.0, block[k : k + 1, :]))
+        row_n = jnp.where(row == n, -1.0, jnp.where(row == k, 0.0, block[n : n + 1, :]))
+        column_k = jnp.where(column == k, -1.0, jnp.where(column == n, 0.0, block[:, k : k + 1]))
+        column_n = jnp.where(column == n, -1.0, jnp.where(column == k, 0.0, block[:, n : n + 1]))
+        solved_k = (c * row_k - b * row_n) * scale
+        solved_n = (a * row_n - b * row_k) * scale
+        outside = (rows // 2 != k // 2) & (columns // 2 != k // 2)
+        block = jnp.where(outside, block, 0.0) - column_k * solved_k - column_n * solved_n
+    out_ref[...] = (-block).astype(bf16)
+
+
+def invert_block(first, second, counted):
+    order = first.shape[0]
     return pl.pallas_call(
         inverse_kernel,
-        out_shape=jax.ShapeDtypeStruct((many, order, order), bf16),
+        out_shape=jax.ShapeDtypeStruct((order, order), bf16),
         in_specs=[
+            pl.BlockSpec(memory_space=pltpu.VMEM),
             pl.BlockSpec(memory_space=pltpu.VMEM),
             pl.BlockSpec(memory_space=pltpu.SMEM),
         ],
         out_specs=pl.BlockSpec(memory_space=pltpu.VMEM),
-        scratch_shapes=[pltpu.VMEM((many, order, order), f32)],
-    )(parts, counted)
+    )(first, second, counted)
 
 
 def swap_cores(array):
@@ -250,12 +219,17 @@
     return lax.ppermute(array, "section", pairs)
 
 
-def groups_along(count, stride, length):
-    return [
-        [base + stride * k for k in range(length)]
-        for base in range(count)
-        if (base // stride) % length == 0
-    ]
+GROUP = 8
+
+
+def groups_near(count):
+    return [list(range(base, base + GROUP)) for base in range(0, count, GROUP)]
+
+
+def swap_groups(array, apart):
+    count = lax.axis_size("dp")
+    pairs = [(i, (i // GROUP ^ apart) * GROUP + i % GROUP) for i in range(count)]
+    return lax.ppermute(array, "dp", pairs)
 
 
 def halves(core, own, other):
@@ -265,39 +239,45 @@
 
 
 def spread(values):
-    lines = groups_along(lax.axis_size("dp"), 4, 8)
+    lines = groups_near(lax.axis_size("dp"))
     return lax.all_to_all(
         values, "dp", split_axis=1, concat_axis=0, axis_index_groups=lines, tiled=True
     )
 
 
 def gather_back(values):
-    lines = groups_along(lax.axis_size("dp"), 4, 8)
+    lines = groups_near(lax.axis_size("dp"))
     return lax.all_to_all(
         values, "dp", split_axis=0, concat_axis=1, axis_index_groups=lines, tiled=True
     )
 
 
-def gram_parts(taken, live):
-    blocks = taken.shape[1] // BLOCK
+def gram_halves(taken, live, odd):
     masked = jnp.where(live, taken, jnp.zeros((), bf16))
     grams = []
-    for b in range(blocks):
+    for b in range(2):
         part = masked[:, b * BLOCK : (b + 1) * BLOCK]
         grams.append(
             lax.dot_general(part, part, (((0,), (0,)), ((), ())), preferred_element_type=f32)
         )
-    mates = groups_along(lax.axis_size("dp"), 1, 4)
-    return lax.all_gather(jnp.stack(grams), "dp", axis=0, axis_index_groups=mates)
-
-
-def apply_blocks(taken, inverse):
-    blocks = inverse.shape[0]
+    mine = jnp.where(odd, grams[1], grams[0])
+    theirs = jnp.where(odd, grams[0], grams[1])
+    return mine, theirs
+
+
+def sum_and_invert(mine, theirs, counted, odd):
+    paired = mine + swap_groups(theirs, 1)
+    inverse = invert_block(paired, swap_groups(paired, 2), counted)
+    other = swap_groups(inverse, 1)
+    return jnp.where(odd, other, inverse), jnp.where(odd, inverse, other)
+
+
+def apply_blocks(taken, inverses):
     results = [
         jnp.dot(
-            taken[:, b * BLOCK : (b + 1) * BLOCK], inverse[b], preferred_element_type=f32
+            taken[:, b * BLOCK : (b + 1) * BLOCK], inverse, preferred_element_type=f32
         ).astype(bf16)
-        for b in range(blocks)
+        for b, inverse in enumerate(inverses)
     ]
     return jnp.concatenate(results, axis=1)
 
@@ -321,8 +301,9 @@
     all_lengths = lax.all_gather(lengths, "dp", axis=0)
     alive = jnp.clip(all_lengths, 0, batch_rows)
     counted = jnp.sum(alive).astype(f32).reshape(1)
-    across = lax.axis_index("dp") % 4
-    line = lax.dynamic_index_in_dim(all_lengths.reshape(8, 4, -1), across, 1, keepdims=False)
+    near = lax.axis_index("dp") // GROUP
+    odd = near % 2 == 1
+    line = lax.dynamic_index_in_dim(all_lengths.reshape(4, GROUP, -1), near, 0, keepdims=False)
     live = (jnp.arange(batch_rows)[None, :] < line.reshape(-1, 1)).reshape(-1, 1)
 
     def own_half(array):
@@ -388,20 +369,20 @@
             mean = jnp.mean(full * full, axis=-1, keepdims=True)
             full = (full * lax.rsqrt(mean + EPSILON)).astype(bf16)
             taken = spread(full)
-            parts = gram_parts(taken, live)
+            parts = gram_halves(taken, live, odd)
             arriving, parts = lax.optimization_barrier((arriving, parts))
         elif stage == chips - 2:
             grads, parts = lax.optimization_barrier((grads, parts))
-            inverse = invert_blocks(parts, counted)
-            pre_inputs = gather_back(apply_blocks(taken, inverse))
+            inverses = sum_and_invert(*parts, counted, odd)
+            pre_inputs = gather_back(apply_blocks(taken, inverses))
             arriving, pre_inputs = lax.optimization_barrier((arriving, pre_inputs))
 
     grad_a, grad_b = grads
     own = jnp.where(core == 0, grad_a, grad_b)
     other = swap_cores(jnp.where(core == 0, grad_b, grad_a))
     taken = spread(halves(core, own, other))
-    inverse = invert_blocks(gram_parts(taken, live), counted)
-    pre_grads = gather_back(apply_blocks(taken, inverse))
+    inverses = sum_and_invert(*gram_halves(taken, live, odd), counted, odd)
+    pre_grads = gather_back(apply_blocks(taken, inverses))
     return (pre_inputs[None], pre_grads[None])
 
 

time: 502 us -> 510 us (1.016)
  the two profiles are of different devices: /device:TPU:2 before, /device:TPU:1 now
where the time goes in v3:
time: 510 us; the launch traced here: 500 us
  waiting for transfers between devices  328 us (64%)
  blocking collectives  52.6 us (10%)
  Pallas kernels  46 us (9%)
  starting transfers between devices  25.8 us (5%)
  between operations  16.3 us (3%)
  local copies, waits for them, and re-layouts  14.5 us (3%)
  other arithmetic  10.4 us (2%)
  matrix products  5.82 us (1%)
    ppermute x6, waiting for transfers between devices, hop(): return lax.ppermute(array, 'section', pairs)  143 us
    all_gather x1, waiting for transfers between devices, all_stages(): weight = lax.all_gather(paired, 'dp', axis=0, tiled=True)  101 us
    ppermute x6, waiting for transfers between devices, swap_groups(): return lax.ppermute(array, 'dp', pairs)  52.2 us
    pallas_call x2, Pallas kernels, invert_block(): pl.pallas_call(inverse_kernel, out_shape=jax.ShapeDtypeStruct((order, ord...  27.5 us
    all_to_all x1, blocking collectives, spread(): lax.all_to_all(values, 'dp', split_axis=1, concat_axis=0, axis_index_grou...  18.9 us
    unnamed x1, blocking collectives  17.4 us
    all_to_all x1, blocking collectives, gather_back(): lax.all_to_all(values, 'dp', split_axis=0, concat_axis=1, axis_index_grou...  16.4 us
    all_to_all x1, waiting for transfers between devices, spread(): lax.all_to_all(values, 'dp', split_axis=1, concat_axis=0, axis_index_grou...  13.4 us
  transfers between devices with their start and end apart: 19, of which 15 were waited for; matrix products, arithmetic and copies ran while one was open for 1% of the time, Pallas kernels for 0%

profile of v3, /device:TPU:1, one launch (start us, length us, event | category | flops | bytes accessed | tf_op | source)
XLA Modules:
  0.0 500.2 jit_solution(8438295714398305268)
XLA Ops:
  8.4 3.3 collective-permute-start.14
  16.2 17.4 %all-reduce = s32[160]{0:T(256)S(1)} all-reduce(s32[160]{0:T(256)S(1)} %dynamic-update-slice), channel_id=2, replica_groups=mesh['section'=8,'dp'=32] {'dp'}, use_global_device_ids=true, to_apply=%add | all-reduce | flops 160 | bytes 1280
  35.3 101.2 %all-gather.3.cloned.1.call-done = bf16[2560,2560]{1,0:T(8,128)(2,1)} async-done(((bf16[80,2560]{1,0:T(8,128)(2,1)}), bf16[2560,2560]{1,0:T(8,128)(2,1)}) %all-gather.3.cloned.1.call-update) | async-done | bytes 13107216 | tf_op jit(solution)/shard_map/all_gather | solution.py:299
  136.5 12.7 %conditional.8 = (bf16[160,1280]{1,0:T(8,128)(2,1)S(1)}, bf16[160,1280]{1,0:T(8,128)(2,1)}, bf16[160,1280]{1,0:T(8,128)(2,1)}, bf16[160,1280]{1,0:T(8,128)(2,1)}, bf16[160,1280]{1,0:T(8,128)(2,1)S(1)}) conditional(s32[]{:T(128)} %convert_element_type.44, () %tuple.76, (s32[]{:T(128)}, bf16[160,2560]{1,0:T(8,128)(2,1)S(1)}, s32[1]{0:T(128)}, ...), branch_computations={%region_1.2_spmd, %region_2.3_spmd} | conditional | flops 2097356800 | bytes 15974490 | solution.py:337
  137.3 4.7 branch_1_fun.18.own_ref
  145.1 4.1 branch_1_fun.19
  150.5 8.7 %collective-permute-done.15 = bf16[160,1280]{1,0:T(8,128)(2,1)S(1)} collective-permute-done((bf16[160,1280]{1,0:T(8,128)(2,1)S(1)}, bf16[160,1280]{1,0:T(8,128)(2,1)S(1)}, u32[]{:S(2)}, u32[]{:S(2)}) %collective-permute-start.15) | collective-permute-done | bytes 409632 | tf_op jit(solution)/shard_map/ppermute | solution.py:219
  167.7 3.6 all-to-all-start
  172.0 13.4 %all-to-all-done = bf16[160,8,320]{2,0,1:T(8,128)(2,1)S(1)} async-done(((bf16[160,8,320]{2,0,1:T(8,128)(2,1)}), bf16[160,8,320]{2,0,1:T(8,128)(2,1)S(1)}, u32[]{:S(2)}, u32[]{:S(2)}) %all-to-all-start) | async-done | bytes 819232 | tf_op jit(solution)/shard_map/all_to_all | solution.py:243
  188.4 8.2 %collective-permute-done.20 = f32[160,160]{1,0:T(8,128)S(1)} collective-permute-done((f32[160,160]{1,0:T(8,128)S(1)}, f32[160,160]{1,0:T(8,128)S(1)}, u32[]{:S(2)}, u32[]{:S(2)}) %collective-permute-start.20) | collective-permute-done | bytes 102432 | tf_op jit(solution)/shard_map/ppermute | solution.py:232
  199.7 10.4 %collective-permute-done.21.second_ref = f32[160,160]{1,0:T(8,128)S(1)} collective-permute-done((f32[160,160]{1,0:T(8,128)S(1)}, f32[160,160]{1,0:T(8,128)S(1)}, u32[]{:S(2)}, u32[]{:S(2)}) %collective-permute-start.21) | collective-permute-done | bytes 102432 | tf_op jit(solution)/shard_map/ppermute | solution.py:232
  210.7 13.7 %shard_map.60 = bf16[160,160]{1,0:T(8,128)(2,1)} custom-call(f32[160,160]{1,0:T(8,128)} %copy-done.11, f32[160,160]{1,0:T(8,128)} %copy-done.13, f32[1]{0:T(128)} %bitcast.2.count_ref), custom_call_target="tpu_custom_call" | custom-call | tf_op jit(solution)/shard_map/pallas_call | solution.py:200
  224.5 6.5 %collective-permute-done.22 = bf16[160,160]{1,0:T(8,128)(2,1)S(1)} collective-permute-done((bf16[160,160]{1,0:T(8,128)(2,1)}, bf16[160,160]{1,0:T(8,128)(2,1)S(1)}, u32[]{:S(2)}, u32[]{:S(2)}) %collective-permute-start.22) | collective-permute-done | bytes 51232 | tf_op jit(solution)/shard_map/ppermute | solution.py:232
  234.2 3.6 all-to-all-start.1
  238.5 13.2 %all-to-all-done.1 = bf16[8,160,320]{2,1,0:T(8,128)(2,1)S(1)} async-done(((bf16[8,160,320]{2,1,0:T(8,128)(2,1)}), bf16[8,160,320]{2,1,0:T(8,128)(2,1)S(1)}, u32[]{:S(2)}, u32[]{:S(2)}) %all-to-all-start.1) | async-done | bytes 819232 | tf_op jit(solution)/shard_map/all_to_all | solution.py:250
  255.1 133.9 %collective-permute-done.23 = bf16[160,1280]{1,0:T(8,128)(2,1)S(1)} collective-permute-done((bf16[160,1280]{1,0:T(8,128)(2,1)S(1)}, bf16[160,1280]{1,0:T(8,128)(2,1)S(1)}, u32[]{:S(2)}, u32[]{:S(2)}) %collective-permute-start.23) | collective-permute-done | bytes 409632 | tf_op jit(solution)/shard_map/ppermute | solution.py:219
  389.0 13.9 %conditional.15 = ((bf16[160,1280]{1,0:T(8,128)(2,1)}, bf16[160,1280]{1,0:T(8,128)(2,1)})) conditional(s32[]{:T(128)} %convert_element_type.44, (bf16[160,1280]{1,0:T(8,128)(2,1)}, bf16[160,1280]{1,0:T(8,128)(2,1)}) %tuple.94, (s32[1]{0:T(128)}, bf16[160,1280]{1,0:T(8,128)(2,1)S(1)}, bf16[160,1280]{1,0:T(8,128)(2,1)}, ...), branch_computations={%region_16.17_spmd, %region_17.18_spmd} | conditional | flops 1050214400 | bytes 17858652 | solution.py:359
  389.0 7.0 %branch_1_fun.34 = (f32[160,1408]{1,0:T(8,128)}, f32[160,1408]{1,0:T(8,128)}) custom-call(s32[1]{0:T(128)} %get-tuple-element.187.core_ref, bf16[160,1280]{1,0:T(8,128)(2,1)S(1)} %get-tuple-element.356.refs_0_.grad_ref, bf16[160,1280]{1,0:T(8,128)(2,1)} %get-tuple-element.188.refs_1_.own_ref, bf16[160,1280]{1,0:T(8,128)(2,1)} %get-tuple-element.189.refs_2_, ...), custom_call_target="tpu_custom_call" | custom-call | flops 1048576000 | bytes 6553600 | tf_op jit(solution)/shard_map/cond/branch_1_fun/pallas_call | solution.py:158
  407.8 18.9 %all_to_all.70 = bf16[160,8,320]{2,0,1:T(8,128)(2,1)S(1)} all-to-all(bf16[160,8,320]{2,0,1:T(8,128)(2,1)S(1)} %copy.18), channel_id=1, replica_groups={{0,1,2,3,4,5,6,7},{8,9,10,11,12,13,14,15},{16,17,18,19,20,21,22,23},{24..., dimensions={1} | all-to-all | bytes 1638400 | tf_op jit(solution)/shard_map/all_to_all | solution.py:243
  428.6 9.4 %collective-permute-done.25 = f32[160,160]{1,0:T(8,128)S(1)} collective-permute-done((f32[160,160]{1,0:T(8,128)S(1)}, f32[160,160]{1,0:T(8,128)S(1)}, u32[]{:S(2)}, u32[]{:S(2)}) %collective-permute-start.25) | collective-permute-done | bytes 102432 | tf_op jit(solution)/shard_map/ppermute | solution.py:232
  439.9 10.4 %collective-permute-done.26.second_ref = f32[160,160]{1,0:T(8,128)S(1)} collective-permute-done((f32[160,160]{1,0:T(8,128)S(1)}, f32[160,160]{1,0:T(8,128)S(1)}, u32[]{:S(2)}, u32[]{:S(2)}) %collective-permute-start.26) | collective-permute-done | bytes 102432 | tf_op jit(solution)/shard_map/ppermute | solution.py:232
  451.0 13.7 %shard_map.61 = bf16[160,160]{1,0:T(8,128)(2,1)} custom-call(f32[160,160]{1,0:T(8,128)} %copy-done.10, f32[160,160]{1,0:T(8,128)} %copy-done.12, f32[1]{0:T(128)} %bitcast.2.count_ref), custom_call_target="tpu_custom_call" | custom-call | tf_op jit(solution)/shard_map/pallas_call | solution.py:200
  465.0 7.2 %collective-permute-done.27 = bf16[160,160]{1,0:T(8,128)(2,1)S(1)} collective-permute-done((bf16[160,160]{1,0:T(8,128)(2,1)}, bf16[160,160]{1,0:T(8,128)(2,1)S(1)}, u32[]{:S(2)}, u32[]{:S(2)}) %collective-permute-start.27) | collective-permute-done | bytes 51232 | tf_op jit(solution)/shard_map/ppermute | solution.py:232
  474.7 16.4 %all_to_all.71 = bf16[8,160,320]{2,1,0:T(8,128)(2,1)S(1)} all-to-all(bf16[8,160,320]{2,1,0:T(8,128)(2,1)S(1)} %bitcast.21), channel_id=1, replica_groups={{0,1,2,3,4,5,6,7},{8,9,10,11,12,13,14,15},{16,17,18,19,20,21,22,23},{24..., dimensions={0} | all-to-all | bytes 1638400 | tf_op jit(solution)/shard_map/all_to_all | solution.py:250
  (107 shorter events, 57.6 us)
Async XLA Ops:
  7.2 7.5 %copy-start.15 = (u32[256]{0:T(256)S(1)}, u32[256]{0:T(256)}, u32[]{:S(2)}) copy-start(u32[256]{0:T(256)} %constant.85) | copy-start | bytes 3076
  7.2 8.8 %copy-start.14 = (s32[5]{0:T(128)S(1)}, s32[5]{0:T(128)}, u32[]{:S(2)}) copy-start(s32[5]{0:T(128)} %param.23) | copy-start | bytes 64
  7.2 28.0 %copy-start.1 = (bf16[160,2560]{1,0:T(8,128)(2,1)S(1)}, bf16[160,2560]{1,0:T(8,128)(2,1)}, u32[]{:S(2)}) copy-start(bf16[160,2560]{1,0:T(8,128)(2,1)} %param.20) | copy-start | bytes 2457604
  7.2 129.3 %all-gather.3.cloned.1.call-start = ((), (), s32[]{:S(2)}) async-start(), calls=%async_computation.4 | async-start | bytes 13516800 | tf_op jit(solution)/shard_map/all_gather | solution.py:299
  8.4 4.4 collective-permute-start.14
  142.0 3.1 collective-permute-start.11
  149.2 10.0 %collective-permute-start.15 = (bf16[160,1280]{1,0:T(8,128)(2,1)S(1)}, bf16[160,1280]{1,0:T(8,128)(2,1)S(1)}, u32[]{:S(2)}, u32[]{:S(2)}) collective-permute-start(bf16[160,1280]{1,0:T(8,128)(2,1)S(1)} %get-tuple-element.244), channel_id=1, source_target_pairs={{0,64},{32,96},{1,65},{33,97},{2,66},{34,98},{3,67},{35,99},{4,68}... | collective-permute-start | bytes 1228808 | tf_op jit(solution)/shard_map/ppermute | solution.py:219
  159.3 0.7 collective-permute-start.16
  160.0 0.7 collective-permute-start.17
  167.7 17.7 %all-to-all-start = ((bf16[160,8,320]{2,0,1:T(8,128)(2,1)}), bf16[160,8,320]{2,0,1:T(8,128)(2,1)S(1)}, u32[]{:S(2)}, u32[]{:S(2)}) async-start(bf16[160,8,320]{2,0,1:T(8,128)(2,1)} %multiply_convert_fusion), calls=%async_computation | async-start | bytes 1966080 | tf_op jit(solution)/shard_map/all_to_all | solution.py:243
  171.3 15.5 %collective-permute-start.18 = (bf16[160,1280]{1,0:T(8,128)(2,1)}, bf16[160,1280]{1,0:T(8,128)(2,1)S(1)}, u32[]{:S(2)}, u32[]{:S(2)}) collective-permute-start(bf16[160,1280]{1,0:T(8,128)(2,1)} %get-tuple-element.261), channel_id=1, source_target_pairs={{192,128},{224,160},{193,129},{225,161},{194,130},{226,162},{195,1... | collective-permute-start | bytes 1228808 | tf_op jit(solution)/shard_map/ppermute | solution.py:219
  186.9 9.7 %collective-permute-start.20 = (f32[160,160]{1,0:T(8,128)S(1)}, f32[160,160]{1,0:T(8,128)S(1)}, u32[]{:S(2)}, u32[]{:S(2)}) collective-permute-start(f32[160,160]{1,0:T(8,128)S(1)} %get-tuple-element.272), channel_id=1, source_target_pairs={{0,8},{1,9},{2,10},{3,11},{4,12},{5,13},{6,14},{7,15},{8,0},{9,1},... | collective-permute-start | bytes 307208 | tf_op jit(solution)/shard_map/ppermute | solution.py:232
  196.6 13.5 %copy-start.11 = (f32[160,160]{1,0:T(8,128)}, f32[160,160]{1,0:T(8,128)S(1)}, u32[]{:S(2)}) copy-start(f32[160,160]{1,0:T(8,128)S(1)} %add.35.first_ref) | copy-start | bytes 307204
  196.6 13.5 %collective-permute-start.21 = (f32[160,160]{1,0:T(8,128)S(1)}, f32[160,160]{1,0:T(8,128)S(1)}, u32[]{:S(2)}, u32[]{:S(2)}) collective-permute-start(f32[160,160]{1,0:T(8,128)S(1)} %add.35.first_ref), channel_id=1, source_target_pairs={{0,16},{1,17},{2,18},{3,19},{4,20},{5,21},{6,22},{7,23},{8,24},{9,... | collective-permute-start | bytes 307208 | tf_op jit(solution)/shard_map/ppermute | solution.py:232
  224.5 6.5 %collective-permute-start.22 = (bf16[160,160]{1,0:T(8,128)(2,1)}, bf16[160,160]{1,0:T(8,128)(2,1)S(1)}, u32[]{:S(2)}, u32[]{:S(2)}) collective-permute-start(bf16[160,160]{1,0:T(8,128)(2,1)} %shard_map.60), channel_id=1, source_target_pairs={{0,8},{1,9},{2,10},{3,11},{4,12},{5,13},{6,14},{7,15},{8,0},{9,1},... | collective-permute-start | bytes 153608 | tf_op jit(solution)/shard_map/ppermute | solution.py:232
  234.2 17.4 %all-to-all-start.1 = ((bf16[8,160,320]{2,1,0:T(8,128)(2,1)}), bf16[8,160,320]{2,1,0:T(8,128)(2,1)S(1)}, u32[]{:S(2)}, u32[]{:S(2)}) async-start(bf16[8,160,320]{2,1,0:T(8,128)(2,1)} %bitcast.7), calls=%async_computation.1 | async-start | bytes 1966080 | tf_op jit(solution)/shard_map/all_to_all | solution.py:250
  237.8 15.7 %collective-permute-start.19 = (bf16[160,1280]{1,0:T(8,128)(2,1)S(1)}, bf16[160,1280]{1,0:T(8,128)(2,1)S(1)}, u32[]{:S(2)}, u32[]{:S(2)}) collective-permute-start(bf16[160,1280]{1,0:T(8,128)(2,1)S(1)} %get-tuple-element.266), channel_id=1, source_target_pairs={{128,64},{160,96},{129,65},{161,97},{130,66},{162,98},{131,67},{16... | collective-permute-start | bytes 1228808 | tf_op jit(solution)/shard_map/ppermute | solution.py:219
  253.8 135.2 %collective-permute-start.23 = (bf16[160,1280]{1,0:T(8,128)(2,1)S(1)}, bf16[160,1280]{1,0:T(8,128)(2,1)S(1)}, u32[]{:S(2)}, u32[]{:S(2)}) collective-permute-start(bf16[160,1280]{1,0:T(8,128)(2,1)S(1)} %get-tuple-element.280), channel_id=1, source_target_pairs={{64,0},{96,32},{65,1},{97,33},{66,2},{98,34},{67,3},{99,35},{68,4}... | collective-permute-start | bytes 1228808 | tf_op jit(solution)/shard_map/ppermute | solution.py:219
  396.0 3.2 collective-permute-start.10
  403.9 1.8 collective-permute-start.24
  428.0 10.0 %collective-permute-start.25 = (f32[160,160]{1,0:T(8,128)S(1)}, f32[160,160]{1,0:T(8,128)S(1)}, u32[]{:S(2)}, u32[]{:S(2)}) collective-permute-start(f32[160,160]{1,0:T(8,128)S(1)} %get-tuple-element.293), channel_id=1, source_target_pairs={{0,8},{1,9},{2,10},{3,11},{4,12},{5,13},{6,14},{7,15},{8,0},{9,1},... | collective-permute-start | bytes 307208 | tf_op jit(solution)/shard_map/ppermute | solution.py:232
  438.0 12.3 %copy-start.10 = (f32[160,160]{1,0:T(8,128)}, f32[160,160]{1,0:T(8,128)S(1)}, u32[]{:S(2)}) copy-start(f32[160,160]{1,0:T(8,128)S(1)} %select_add_fusion.first_ref) | copy-start | bytes 307204
  438.0 12.3 %collective-permute-start.26 = (f32[160,160]{1,0:T(8,128)S(1)}, f32[160,160]{1,0:T(8,128)S(1)}, u32[]{:S(2)}, u32[]{:S(2)}) collective-permute-start(f32[160,160]{1,0:T(8,128)S(1)} %select_add_fusion.first_ref), channel_id=1, source_target_pairs={{0,16},{1,17},{2,18},{3,19},{4,20},{5,21},{6,22},{7,23},{8,24},{9,... | collective-permute-start | bytes 307208 | tf_op jit(solution)/shard_map/ppermute | solution.py:232
  464.7 7.4 %collective-permute-start.27 = (bf16[160,160]{1,0:T(8,128)(2,1)}, bf16[160,160]{1,0:T(8,128)(2,1)S(1)}, u32[]{:S(2)}, u32[]{:S(2)}) collective-permute-start(bf16[160,160]{1,0:T(8,128)(2,1)} %shard_map.61), channel_id=1, source_target_pairs={{0,8},{1,9},{2,10},{3,11},{4,12},{5,13},{6,14},{7,15},{8,0},{9,1},... | collective-permute-start | bytes 153608 | tf_op jit(solution)/shard_map/ppermute | solution.py:232
  (4 other events, 3.7 us)
Sparse Core Ops, SparseCore 0:
  14.8 121.6 all-gather.2

commit v4 on v3

--- a/solution.py
+++ b/solution.py
@@ -68,46 +68,44 @@
     )(core, own, other, weight, weight)
 
 
-def finish(grad, keep, sent, arrived, own):
+def finish(grad, keep, arrived, own):
     half = own.shape[1]
-    mean = jnp.sum(sent + arrived[:, half:], axis=-1, keepdims=True) / (2 * half)
+    mine, theirs = keep[:, half + LANES :], arrived[:, half:].astype(f32)
+    mean = jnp.sum(mine + theirs, axis=-1, keepdims=True) / (2 * half)
     factor = keep[:, half : half + 1]
-    back = keep[:, :half] + arrived[:, :half]
+    back = keep[:, :half] + arrived[:, :half].astype(f32)
     through = factor * (back - own.astype(f32) * factor * mean)
     return (grad.astype(f32) + through).astype(bf16)
 
 
-def finish_kernel(grad_ref, keep_ref, sent_ref, arrived_ref, own_ref, out_ref):
-    out_ref[...] = finish(
-        grad_ref[...], keep_ref[...], sent_ref[...], arrived_ref[...], own_ref[...]
-    )
-
-
-def finish_layer(grad, keep, send, arrived, own):
+def finish_kernel(grad_ref, keep_ref, arrived_ref, own_ref, out_ref):
+    out_ref[...] = finish(grad_ref[...], keep_ref[...], arrived_ref[...], own_ref[...])
+
+
+def finish_layer(grad, keep, arrived, own):
     rows, half = own.shape
-    whole = pl.BlockSpec((rows, half), lambda i: (0, 0))
-    wide = pl.BlockSpec((rows, half + LANES), lambda i: (0, 0))
+    whole = pl.BlockSpec(memory_space=pltpu.VMEM)
     return pl.pallas_call(
         finish_kernel,
         out_shape=jax.ShapeDtypeStruct((rows, half), bf16),
-        grid=(1,),
-        in_specs=[whole, wide, pl.BlockSpec((rows, LANES), lambda i: (0, half // LANES)), wide, whole],
+        in_specs=[whole] * 4,
         out_specs=whole,
         cost_estimate=pl.CostEstimate(
             flops=8 * rows * half, bytes_accessed=16 * rows * half, transcendentals=0
         ),
-    )(grad, keep, send, arrived, own)
+    )(grad, keep, arrived, own)
 
 
 def backward_kernel(fused, core_ref, *refs):
     if fused:
-        before, refs = refs[:5], refs[5:]
+        before, refs = refs[:4], refs[4:]
         own_ref, other_ref, weight_ref, send_ref, keep_ref, grad_ref = refs
     else:
         grad_ref, own_ref, other_ref, weight_ref, send_ref, keep_ref = refs
     step = pl.program_id(0)
     rows, half = own_ref.shape
     steps = half // ROWS
+    factor_at, product_at = slice(half, half + LANES), slice(half + LANES, half + 2 * LANES)
 
     @pl.when(step == 0)
     def _():
@@ -115,8 +113,8 @@
             grad_ref[...] = finish(*[ref[...] for ref in before])
         own = own_ref[...].astype(f32)
         other = other_ref[...].astype(f32)
-        keep_ref[:, half:] = jnp.broadcast_to(row_factor(own, other, 2 * half), (rows, LANES))
-        send_ref[:, half:] = jnp.zeros((rows, LANES), f32)
+        keep_ref[:, factor_at] = jnp.broadcast_to(row_factor(own, other, 2 * half), (rows, LANES))
+        keep_ref[:, product_at] = jnp.zeros((rows, LANES), f32)
 
     part = lax.dot_general(
         grad_ref[...], weight_ref[...], (((1,), (1,)), ((), ())), preferred_element_type=f32
@@ -127,12 +125,12 @@
         folded = product[:, :LANES]
         for k in range(1, ROWS // LANES):
             folded = folded + product[:, k * LANES : (k + 1) * LANES]
-        send_ref[:, half:] += folded * keep_ref[:, half:]
+        keep_ref[:, product_at] += folded * keep_ref[:, factor_at]
 
     @pl.when(step < steps)
     def _():
         columns = pl.ds(pl.multiple_of(step * ROWS, LANES), ROWS)
-        send_ref[:, columns] = part
+        send_ref[:, columns] = part.astype(bf16)
         along(other_ref, columns)
 
     @pl.when(step >= steps)
@@ -140,29 +138,36 @@
         columns = pl.ds(pl.multiple_of((step - steps) * ROWS, LANES), ROWS)
         keep_ref[:, columns] = part
         along(own_ref, columns)
+
+    @pl.when(step == 2 * steps - 1)
+    def _():
+        send_ref[:, half:] = keep_ref[:, product_at].astype(bf16)
 
 
 def backward_layer(core, before, own, other, weight, which):
     rows, half = own.shape
     steps = half // ROWS
     fused = len(before) > 1
-    whole = pl.BlockSpec((rows, half), lambda i, c: (0, 0))
-    wide = pl.BlockSpec((rows, half + LANES), lambda i, c: (0, 0))
-    tail = pl.BlockSpec((rows, LANES), lambda i, c: (0, half // LANES))
+
+    def whole(extra=0):
+        return pl.BlockSpec((rows, half + extra), lambda i, c: (0, 0))
 
     def place(i, c):
         return (jnp.where(i < steps, (1 - c[0]) * steps + i, c[0] * steps + i - steps), which)
 
-    out_shape = [jax.ShapeDtypeStruct((rows, half + LANES), f32)] * 2
-    first = [whole, wide, tail, wide, whole] if fused else [whole]
+    out_shape = [
+        jax.ShapeDtypeStruct((rows, half + LANES), bf16),
+        jax.ShapeDtypeStruct((rows, half + 2 * LANES), f32),
+    ]
+    first = [whole(), whole(2 * LANES), whole(LANES), whole()] if fused else [whole()]
     results = pl.pallas_call(
         functools.partial(backward_kernel, fused),
         out_shape=out_shape + [jax.ShapeDtypeStruct((rows, half), bf16)] * fused,
         grid_spec=pltpu.PrefetchScalarGridSpec(
             num_scalar_prefetch=1,
             grid=(2 * steps,),
-            in_specs=first + [whole, whole, pl.BlockSpec((ROWS, half), place)],
-            out_specs=[wide, wide] + [whole] * fused,
+            in_specs=first + [whole(), whole(), pl.BlockSpec((ROWS, half), place)],
+            out_specs=[whole(LANES), whole(2 * LANES)] + [whole()] * fused,
         ),
         cost_estimate=pl.CostEstimate(
             flops=4 * rows * half * half, bytes_accessed=4 * half * half, transcendentals=0
@@ -170,15 +175,16 @@
     )(core, *before, own, other, weight)
     send, keep = results[:2]
     grad = results[2] if fused else before[0]
-    return (grad, keep, send, swap_cores(send), own)
-
-
-def inverse_kernel(first_ref, second_ref, count_ref, out_ref):
+    return (grad, keep, swap_cores(send), own)
+
+
+def inverse_kernel(first_ref, second_ref, third_ref, fourth_ref, count_ref, out_ref):
     order = out_ref.shape[0]
     rows = lax.broadcasted_iota(jnp.int32, (order, order), 0)
     columns = lax.broadcasted_iota(jnp.int32, (order, order), 1)
     row, column = columns[:1], rows[:, :1]
-    block = (first_ref[...] + second_ref[...]) / count_ref[0]
+    block = (first_ref[...] + second_ref[...]) + (third_ref[...] + fourth_ref[...])
+    block = block / count_ref[0]
     block = block + jnp.where(rows == columns, DAMPING, 0.0)
     for k in range(0, order, 2):
         n = k + 1
@@ -195,18 +201,17 @@
     out_ref[...] = (-block).astype(bf16)
 
 
-def invert_block(first, second, counted):
-    order = first.shape[0]
+def invert_block(parts, counted):
+    order = parts[0].shape[0]
     return pl.pallas_call(
         inverse_kernel,
         out_shape=jax.ShapeDtypeStruct((order, order), bf16),
         in_specs=[
-            pl.BlockSpec(memory_space=pltpu.VMEM),
-            pl.BlockSpec(memory_space=pltpu.VMEM),
+            *[pl.BlockSpec(memory_space=pltpu.VMEM)] * 4,
             pl.BlockSpec(memory_space=pltpu.SMEM),
         ],
         out_specs=pl.BlockSpec(memory_space=pltpu.VMEM),
-    )(first, second, counted)
+    )(*parts, counted)
 
 
 def swap_cores(array):
@@ -266,8 +271,8 @@
 
 
 def sum_and_invert(mine, theirs, counted, odd):
-    paired = mine + swap_groups(theirs, 1)
-    inverse = invert_block(paired, swap_groups(paired, 2), counted)
+    parts = (mine, swap_groups(theirs, 1), swap_groups(mine, 2), swap_groups(theirs, 3))
+    inverse = invert_block(parts, counted)
     other = swap_groups(inverse, 1)
     return jnp.where(odd, other, inverse), jnp.where(odd, inverse, other)
 

time: 510 us -> 492 us (0.965)
  the two profiles are of different devices: /device:TPU:1 before, /device:TPU:2 now
where the time goes in v4:
time: 492 us; the launch traced here: 482 us
  waiting for transfers between devices  301 us (61%)
  blocking collectives  57 us (12%)
  Pallas kernels  46 us (9%)
  starting transfers between devices  31.4 us (6%)
  between operations  16.3 us (3%)
  local copies, waits for them, and re-layouts  14.1 us (3%)
  other arithmetic  10.1 us (2%)
  matrix products  5.82 us (1%)
    ppermute x6, waiting for transfers between devices, hop(): return lax.ppermute(array, 'section', pairs)  136 us
    all_gather x1, waiting for transfers between devices, all_stages(): weight = lax.all_gather(paired, 'dp', axis=0, tiled=True)  97.5 us
    ppermute x8, waiting for transfers between devices, swap_groups(): return lax.ppermute(array, 'dp', pairs)  37.1 us
    pallas_call x2, Pallas kernels, invert_block(): pl.pallas_call(inverse_kernel, out_shape=jax.ShapeDtypeStruct((order, ord...  27.8 us
    unnamed x1, blocking collectives  22.6 us
    all_to_all x1, blocking collectives, spread(): lax.all_to_all(values, 'dp', split_axis=1, concat_axis=0, axis_index_grou...  19.1 us
    ppermute x8, starting transfers between devices, swap_groups(): return lax.ppermute(array, 'dp', pairs)  16 us
    all_to_all x1, blocking collectives, gather_back(): lax.all_to_all(values, 'dp', split_axis=0, concat_axis=1, axis_index_grou...  15.3 us
  transfers between devices with their start and end apart: 21, of which 16 were waited for; matrix products, arithmetic and copies ran while one was open for 1% of the time, Pallas kernels for 0%

profile of v4, /device:TPU:2, one launch (start us, length us, event | category | flops | bytes accessed | tf_op | source)
XLA Modules:
  0.0 482.3 jit_solution(13536551745464033908)
XLA Ops:
  13.4 22.6 %all-reduce = s32[160]{0:T(256)S(1)} all-reduce(s32[160]{0:T(256)S(1)} %dynamic-update-slice), channel_id=2, replica_groups=mesh['section'=8,'dp'=32] {'dp'}, use_global_device_ids=true, to_apply=%add | all-reduce | flops 160 | bytes 1280
  37.6 97.5 %all-gather.3.cloned.1.call-done = bf16[2560,2560]{1,0:T(8,128)(2,1)} async-done(((bf16[80,2560]{1,0:T(8,128)(2,1)}), bf16[2560,2560]{1,0:T(8,128)(2,1)}) %all-gather.3.cloned.1.call-update) | async-done | bytes 13107216 | tf_op jit(solution)/shard_map/all_gather | solution.py:304
  135.1 11.7 %conditional.8 = (bf16[160,1280]{1,0:T(8,128)(2,1)S(1)}, bf16[160,1280]{1,0:T(8,128)(2,1)}, bf16[160,1280]{1,0:T(8,128)(2,1)}, bf16[160,1280]{1,0:T(8,128)(2,1)}, bf16[160,1280]{1,0:T(8,128)(2,1)S(1)}) conditional(s32[]{:T(128)} %convert_element_type.44, () %tuple.76, (s32[]{:T(128)}, bf16[160,2560]{1,0:T(8,128)(2,1)S(1)}, s32[1]{0:T(128)}, ...), branch_computations={%region_1.2_spmd, %region_2.3_spmd} | conditional | flops 2097356800 | bytes 15974490 | solution.py:342
  135.9 4.6 branch_1_fun.18.own_ref
  142.7 4.1 branch_1_fun.19
  148.1 9.3 %collective-permute-done.15 = bf16[160,1280]{1,0:T(8,128)(2,1)S(1)} collective-permute-done((bf16[160,1280]{1,0:T(8,128)(2,1)S(1)}, bf16[160,1280]{1,0:T(8,128)(2,1)S(1)}, u32[]{:S(2)}, u32[]{:S(2)}) %collective-permute-start.15) | collective-permute-done | bytes 409632 | tf_op jit(solution)/shard_map/ppermute | solution.py:224
  165.0 5.2 %all-to-all-start = ((bf16[160,8,320]{2,0,1:T(8,128)(2,1)}), bf16[160,8,320]{2,0,1:T(8,128)(2,1)S(1)}, u32[]{:S(2)}, u32[]{:S(2)}) async-start(bf16[160,8,320]{2,0,1:T(8,128)(2,1)} %multiply_convert_fusion), calls=%async_computation | async-start | bytes 1966080 | tf_op jit(solution)/shard_map/all_to_all | solution.py:248
  171.0 12.4 %all-to-all-done = bf16[160,8,320]{2,0,1:T(8,128)(2,1)S(1)} async-done(((bf16[160,8,320]{2,0,1:T(8,128)(2,1)}), bf16[160,8,320]{2,0,1:T(8,128)(2,1)S(1)}, u32[]{:S(2)}, u32[]{:S(2)}) %all-to-all-start) | async-done | bytes 819232 | tf_op jit(solution)/shard_map/all_to_all | solution.py:248
  185.3 3.1 collective-permute-start.21
  192.0 6.6 %collective-permute-done.21.third_ref = f32[160,160]{1,0:T(8,128)S(1)} collective-permute-done((f32[160,160]{1,0:T(8,128)S(1)}, f32[160,160]{1,0:T(8,128)S(1)}, u32[]{:S(2)}, u32[]{:S(2)}) %collective-permute-start.21) | collective-permute-done | bytes 102432 | tf_op jit(solution)/shard_map/ppermute | solution.py:237
  198.6 4.9 %collective-permute-done.22.fourth_ref = f32[160,160]{1,0:T(8,128)S(1)} collective-permute-done((f32[160,160]{1,0:T(8,128)S(1)}, f32[160,160]{1,0:T(8,128)S(1)}, u32[]{:S(2)}, u32[]{:S(2)}) %collective-permute-start.22) | collective-permute-done | bytes 102432 | tf_op jit(solution)/shard_map/ppermute | solution.py:237
  206.1 13.9 %shard_map.60 = bf16[160,160]{1,0:T(8,128)(2,1)} custom-call(f32[160,160]{1,0:T(8,128)} %copy-done.10, f32[160,160]{1,0:T(8,128)} %copy-done.17, f32[160,160]{1,0:T(8,128)} %copy-done.13, f32[160,160]{1,0:T(8,128)} %copy-done.15, f32[1]{0:T(128)} %bitcast.2.count_ref), custom_call_target="tpu_custom_call" | custom-call | tf_op jit(solution)/shard_map/pallas_call | solution.py:206
  222.6 4.7 collective-permute-done.23
  230.5 4.4 all-to-all-start.1
  235.6 11.2 %all-to-all-done.1 = bf16[8,160,320]{2,1,0:T(8,128)(2,1)S(1)} async-done(((bf16[8,160,320]{2,1,0:T(8,128)(2,1)}), bf16[8,160,320]{2,1,0:T(8,128)(2,1)S(1)}, u32[]{:S(2)}, u32[]{:S(2)}) %all-to-all-start.1) | async-done | bytes 819232 | tf_op jit(solution)/shard_map/all_to_all | solution.py:255
  250.2 127.1 %collective-permute-done.24 = bf16[160,1280]{1,0:T(8,128)(2,1)S(1)} collective-permute-done((bf16[160,1280]{1,0:T(8,128)(2,1)S(1)}, bf16[160,1280]{1,0:T(8,128)(2,1)S(1)}, u32[]{:S(2)}, u32[]{:S(2)}) %collective-permute-start.24) | collective-permute-done | bytes 409632 | tf_op jit(solution)/shard_map/ppermute | solution.py:224
  377.3 12.2 %conditional.15 = ((bf16[160,1280]{1,0:T(8,128)(2,1)}, bf16[160,1280]{1,0:T(8,128)(2,1)})) conditional(s32[]{:T(128)} %convert_element_type.44, (bf16[160,1280]{1,0:T(8,128)(2,1)}, bf16[160,1280]{1,0:T(8,128)(2,1)}) %tuple.94, (s32[1]{0:T(128)}, bf16[160,1280]{1,0:T(8,128)(2,1)S(1)}, bf16[160,1280]{1,0:T(8,128)(2,1)}, ...), branch_computations={%region_16.17_spmd, %region_17.18_spmd} | conditional | flops 1050214400 | bytes 14254172 | solution.py:364
  377.3 6.8 %branch_1_fun.34 = (bf16[160,1408]{1,0:T(8,128)(2,1)}, f32[160,1536]{1,0:T(8,128)}) custom-call(s32[1]{0:T(128)} %get-tuple-element.187.core_ref, bf16[160,1280]{1,0:T(8,128)(2,1)S(1)} %get-tuple-element.356.refs_0_.grad_ref, bf16[160,1280]{1,0:T(8,128)(2,1)} %get-tuple-element.188.refs_1_.own_ref, bf16[160,1280]{1,0:T(8,128)(2,1)} %get-tuple-element.189.refs_2_, ...), custom_call_target="tpu_custom_call" | custom-call | flops 1048576000 | bytes 6553600 | tf_op jit(solution)/shard_map/cond/branch_1_fun/pallas_call | solution.py:163
  394.4 19.1 %all_to_all.70 = bf16[160,8,320]{2,0,1:T(8,128)(2,1)S(1)} all-to-all(bf16[160,8,320]{2,0,1:T(8,128)(2,1)S(1)} %copy.18), channel_id=1, replica_groups={{0,1,2,3,4,5,6,7},{8,9,10,11,12,13,14,15},{16,17,18,19,20,21,22,23},{24..., dimensions={1} | all-to-all | bytes 1638400 | tf_op jit(solution)/shard_map/all_to_all | solution.py:248
  421.7 6.0 %collective-permute-done.28.fourth_ref = f32[160,160]{1,0:T(8,128)S(1)} collective-permute-done((f32[160,160]{1,0:T(8,128)S(1)}, f32[160,160]{1,0:T(8,128)S(1)}, u32[]{:S(2)}, u32[]{:S(2)}) %collective-permute-start.28) | collective-permute-done | bytes 102432 | tf_op jit(solution)/shard_map/ppermute | solution.py:237
  427.7 7.0 %collective-permute-done.27.third_ref = f32[160,160]{1,0:T(8,128)S(1)} collective-permute-done((f32[160,160]{1,0:T(8,128)S(1)}, f32[160,160]{1,0:T(8,128)S(1)}, u32[]{:S(2)}, u32[]{:S(2)}) %collective-permute-start.27) | collective-permute-done | bytes 102432 | tf_op jit(solution)/shard_map/ppermute | solution.py:237
  435.4 13.9 %shard_map.61 = bf16[160,160]{1,0:T(8,128)(2,1)} custom-call(f32[160,160]{1,0:T(8,128)} %copy-done.11, f32[160,160]{1,0:T(8,128)} %copy-done.14, f32[160,160]{1,0:T(8,128)} %copy-done.16, f32[160,160]{1,0:T(8,128)} %copy-done.12, f32[1]{0:T(128)} %bitcast.2.count_ref), custom_call_target="tpu_custom_call" | custom-call | tf_op jit(solution)/shard_map/pallas_call | solution.py:206
  449.3 6.0 %collective-permute-done.29 = bf16[160,160]{1,0:T(8,128)(2,1)S(1)} collective-permute-done((bf16[160,160]{1,0:T(8,128)(2,1)}, bf16[160,160]{1,0:T(8,128)(2,1)S(1)}, u32[]{:S(2)}, u32[]{:S(2)}) %collective-permute-start.29) | collective-permute-done | bytes 51232 | tf_op jit(solution)/shard_map/ppermute | solution.py:237
  457.8 15.3 %all_to_all.71 = bf16[8,160,320]{2,1,0:T(8,128)(2,1)S(1)} all-to-all(bf16[8,160,320]{2,1,0:T(8,128)(2,1)S(1)} %bitcast.21), channel_id=1, replica_groups={{0,1,2,3,4,5,6,7},{8,9,10,11,12,13,14,15},{16,17,18,19,20,21,22,23},{24..., dimensions={0} | all-to-all | bytes 1638400 | tf_op jit(solution)/shard_map/all_to_all | solution.py:255
  (117 shorter events, 62.0 us)
Async XLA Ops:
  7.2 30.4 %copy-start.1 = (bf16[160,2560]{1,0:T(8,128)(2,1)S(1)}, bf16[160,2560]{1,0:T(8,128)(2,1)}, u32[]{:S(2)}) copy-start(bf16[160,2560]{1,0:T(8,128)(2,1)} %param.20) | copy-start | bytes 2457604
  7.2 127.9 %all-gather.3.cloned.1.call-start = ((), (), s32[]{:S(2)}) async-start(), calls=%async_computation.4 | async-start | bytes 13516800 | tf_op jit(solution)/shard_map/all_gather | solution.py:304
  8.4 1.5 collective-permute-start.14
  140.6 2.1 collective-permute-start.11
  146.8 10.6 %collective-permute-start.15 = (bf16[160,1280]{1,0:T(8,128)(2,1)S(1)}, bf16[160,1280]{1,0:T(8,128)(2,1)S(1)}, u32[]{:S(2)}, u32[]{:S(2)}) collective-permute-start(bf16[160,1280]{1,0:T(8,128)(2,1)S(1)} %get-tuple-element.244), channel_id=1, source_target_pairs={{0,64},{32,96},{1,65},{33,97},{2,66},{34,98},{3,67},{35,99},{4,68}... | collective-permute-start | bytes 1228808 | tf_op jit(solution)/shard_map/ppermute | solution.py:224
  157.4 0.7 collective-permute-start.16
  158.2 0.7 collective-permute-start.17
  165.0 18.3 %all-to-all-start = ((bf16[160,8,320]{2,0,1:T(8,128)(2,1)}), bf16[160,8,320]{2,0,1:T(8,128)(2,1)S(1)}, u32[]{:S(2)}, u32[]{:S(2)}) async-start(bf16[160,8,320]{2,0,1:T(8,128)(2,1)} %multiply_convert_fusion), calls=%async_computation | async-start | bytes 1966080 | tf_op jit(solution)/shard_map/all_to_all | solution.py:248
  170.3 14.4 %collective-permute-start.18 = (bf16[160,1280]{1,0:T(8,128)(2,1)S(1)}, bf16[160,1280]{1,0:T(8,128)(2,1)S(1)}, u32[]{:S(2)}, u32[]{:S(2)}) collective-permute-start(bf16[160,1280]{1,0:T(8,128)(2,1)S(1)} %get-tuple-element.261), channel_id=1, source_target_pairs={{192,128},{224,160},{193,129},{225,161},{194,130},{226,162},{195,1... | collective-permute-start | bytes 1228808 | tf_op jit(solution)/shard_map/ppermute | solution.py:224
  185.3 13.2 %collective-permute-start.21 = (f32[160,160]{1,0:T(8,128)S(1)}, f32[160,160]{1,0:T(8,128)S(1)}, u32[]{:S(2)}, u32[]{:S(2)}) collective-permute-start(f32[160,160]{1,0:T(8,128)S(1)} %get-tuple-element.271.first_ref), channel_id=1, source_target_pairs={{0,16},{1,17},{2,18},{3,19},{4,20},{5,21},{6,22},{7,23},{8,24},{9,... | collective-permute-start | bytes 307208 | tf_op jit(solution)/shard_map/ppermute | solution.py:237
  188.4 15.1 %collective-permute-start.22 = (f32[160,160]{1,0:T(8,128)S(1)}, f32[160,160]{1,0:T(8,128)S(1)}, u32[]{:S(2)}, u32[]{:S(2)}) collective-permute-start(f32[160,160]{1,0:T(8,128)S(1)} %get-tuple-element.272), channel_id=1, source_target_pairs={{0,24},{1,25},{2,26},{3,27},{4,28},{5,29},{6,30},{7,31},{8,16},{9,... | collective-permute-start | bytes 307208 | tf_op jit(solution)/shard_map/ppermute | solution.py:237
  190.9 14.6 %collective-permute-start.20 = (f32[160,160]{1,0:T(8,128)S(1)}, f32[160,160]{1,0:T(8,128)S(1)}, u32[]{:S(2)}, u32[]{:S(2)}) collective-permute-start(f32[160,160]{1,0:T(8,128)S(1)} %get-tuple-element.272), channel_id=1, source_target_pairs={{0,8},{1,9},{2,10},{3,11},{4,12},{5,13},{6,14},{7,15},{8,0},{9,1},... | collective-permute-start | bytes 307208 | tf_op jit(solution)/shard_map/ppermute | solution.py:237
  220.0 7.2 %collective-permute-start.23 = (bf16[160,160]{1,0:T(8,128)(2,1)}, bf16[160,160]{1,0:T(8,128)(2,1)S(1)}, u32[]{:S(2)}, u32[]{:S(2)}) collective-permute-start(bf16[160,160]{1,0:T(8,128)(2,1)} %shard_map.60), channel_id=1, source_target_pairs={{0,8},{1,9},{2,10},{3,11},{4,12},{5,13},{6,14},{7,15},{8,0},{9,1},... | collective-permute-start | bytes 153608 | tf_op jit(solution)/shard_map/ppermute | solution.py:237
  230.5 16.3 %all-to-all-start.1 = ((bf16[8,160,320]{2,1,0:T(8,128)(2,1)}), bf16[8,160,320]{2,1,0:T(8,128)(2,1)S(1)}, u32[]{:S(2)}, u32[]{:S(2)}) async-start(bf16[8,160,320]{2,1,0:T(8,128)(2,1)} %bitcast.7), calls=%async_computation.1 | async-start | bytes 1966080 | tf_op jit(solution)/shard_map/all_to_all | solution.py:255
  234.9 13.7 %collective-permute-start.19 = (bf16[160,1280]{1,0:T(8,128)(2,1)S(1)}, bf16[160,1280]{1,0:T(8,128)(2,1)S(1)}, u32[]{:S(2)}, u32[]{:S(2)}) collective-permute-start(bf16[160,1280]{1,0:T(8,128)(2,1)S(1)} %get-tuple-element.266), channel_id=1, source_target_pairs={{128,64},{160,96},{129,65},{161,97},{130,66},{162,98},{131,67},{16... | collective-permute-start | bytes 1228808 | tf_op jit(solution)/shard_map/ppermute | solution.py:224
  248.9 128.4 %collective-permute-start.24 = (bf16[160,1280]{1,0:T(8,128)(2,1)S(1)}, bf16[160,1280]{1,0:T(8,128)(2,1)S(1)}, u32[]{:S(2)}, u32[]{:S(2)}) collective-permute-start(bf16[160,1280]{1,0:T(8,128)(2,1)S(1)} %get-tuple-element.280), channel_id=1, source_target_pairs={{64,0},{96,32},{65,1},{97,33},{66,2},{98,34},{67,3},{99,35},{68,4}... | collective-permute-start | bytes 1228808 | tf_op jit(solution)/shard_map/ppermute | solution.py:224
  384.1 2.0 collective-permute-start.10
  390.5 1.8 collective-permute-start.25
  414.8 19.9 %copy-start.11 = (f32[160,160]{1,0:T(8,128)}, f32[160,160]{1,0:T(8,128)S(1)}, u32[]{:S(2)}) copy-start(f32[160,160]{1,0:T(8,128)S(1)} %get-tuple-element.292.first_ref) | copy-start | bytes 307204
  414.8 12.8 %collective-permute-start.28 = (f32[160,160]{1,0:T(8,128)S(1)}, f32[160,160]{1,0:T(8,128)S(1)}, u32[]{:S(2)}, u32[]{:S(2)}) collective-permute-start(f32[160,160]{1,0:T(8,128)S(1)} %get-tuple-element.291), channel_id=1, source_target_pairs={{0,24},{1,25},{2,26},{3,27},{4,28},{5,29},{6,30},{7,31},{8,16},{9,... | collective-permute-start | bytes 307208 | tf_op jit(solution)/shard_map/ppermute | solution.py:237
  416.5 11.1 %collective-permute-start.26 = (f32[160,160]{1,0:T(8,128)S(1)}, f32[160,160]{1,0:T(8,128)S(1)}, u32[]{:S(2)}, u32[]{:S(2)}) collective-permute-start(f32[160,160]{1,0:T(8,128)S(1)} %get-tuple-element.291), channel_id=1, source_target_pairs={{0,8},{1,9},{2,10},{3,11},{4,12},{5,13},{6,14},{7,15},{8,0},{9,1},... | collective-permute-start | bytes 307208 | tf_op jit(solution)/shard_map/ppermute | solution.py:237
  418.8 15.9 %collective-permute-start.27 = (f32[160,160]{1,0:T(8,128)S(1)}, f32[160,160]{1,0:T(8,128)S(1)}, u32[]{:S(2)}, u32[]{:S(2)}) collective-permute-start(f32[160,160]{1,0:T(8,128)S(1)} %get-tuple-element.292.first_ref), channel_id=1, source_target_pairs={{0,16},{1,17},{2,18},{3,19},{4,20},{5,21},{6,22},{7,23},{8,24},{9,... | collective-permute-start | bytes 307208 | tf_op jit(solution)/shard_map/ppermute | solution.py:237
  427.7 7.0 %copy-start.12 = (f32[160,160]{1,0:T(8,128)}, f32[160,160]{1,0:T(8,128)S(1)}, u32[]{:S(2)}) copy-start(f32[160,160]{1,0:T(8,128)S(1)} %collective-permute-done.28.fourth_ref) | copy-start | bytes 307204
  449.3 6.0 %collective-permute-start.29 = (bf16[160,160]{1,0:T(8,128)(2,1)}, bf16[160,160]{1,0:T(8,128)(2,1)S(1)}, u32[]{:S(2)}, u32[]{:S(2)}) collective-permute-start(bf16[160,160]{1,0:T(8,128)(2,1)} %shard_map.61), channel_id=1, source_target_pairs={{0,8},{1,9},{2,10},{3,11},{4,12},{5,13},{6,14},{7,15},{8,0},{9,1},... | collective-permute-start | bytes 153608 | tf_op jit(solution)/shard_map/ppermute | solution.py:237
  (10 other events, 30.5 us)
Sparse Core Ops, SparseCore 0:
  11.9 123.1 all-gather.2
